TPU v7x, 32 devices: a whole 2x2x4 slice. The times are simulated.
32 devices in a mesh: row: 16 (over z, y, x), tok: 2 (over core).
Axes of the slice: x: 2, y: 2, z: 4, core: 2. Of those that a mesh axis runs over, the one named last changes fastest.
Arguments:
- tokens: bfloat16 [16, 512, 768], P('row', 'tok'), may hold values from -6 to 6
- cotangent: bfloat16 [16, 512, 768], P('row', 'tok'), may hold values from -6 to 6
- segment_ids: int32 [16, 512], P('row', 'tok'), may hold values from 0 to 5, never falling along the last dimension, each value on 1 to 256 neighbouring positions
- valid: int32 [16, 512], P('row', 'tok'), may hold values from 0 to 1, as said below
- first_gain: float32 [2, 768], replicated, may hold values from 0.5 to 1.5
- first_shift: float32 [2, 768], replicated, may hold values from -2 to 2
- joint_weight: bfloat16 [2, 768, 2304], replicated, may hold values from -0.21875 to 0.21875
- joint_bias: float32 [2, 2, 768], replicated, may hold values from -2 to 2
- output_weight: bfloat16 [2, 768, 768], replicated, may hold values from -1.25 to 1.25
- output_bias: float32 [2, 768], replicated, may hold values from -2 to 2
- second_gain: float32 [2, 768], replicated, may hold values from 0.5 to 1.5
- second_shift: float32 [2, 768], replicated, may hold values from -2 to 2
- up_weight: bfloat16 [2, 768, 3072], replicated, may hold values from -0.21875 to 0.21875
- up_bias: float32 [2, 3072], replicated, may hold values from -2 to 2
- down_weight: bfloat16 [2, 3072, 768], replicated, may hold values from -0.109375 to 0.109375
- down_bias: float32 [2, 768], replicated, may hold values from -2 to 2
Outputs:
- output: bfloat16 [16, 512, 768], P('row', 'tok')
- input_gradient: float32 [16, 512, 768], P('row', 'tok')
- first_gain_gradient: float32 [2, 768], P(None, ('row', 'tok'))
- first_shift_gradient: float32 [2, 768], P(None, ('row', 'tok'))
- joint_weight_gradient: float32 [2, 768, 2304], P(None, ('row', 'tok'))
- joint_bias_gradient: float32 [2, 2, 768], P(None, None, ('row', 'tok'))
- output_weight_gradient: float32 [2, 768, 768], P(None, ('row', 'tok'))
- output_bias_gradient: float32 [2, 768], P(None, ('row', 'tok'))
- second_gain_gradient: float32 [2, 768], P(None, ('row', 'tok'))
- second_shift_gradient: float32 [2, 768], P(None, ('row', 'tok'))
- up_weight_gradient: float32 [2, 768, 3072], P(None, ('row', 'tok'))
- up_bias_gradient: float32 [2, 3072], P(None, ('row', 'tok'))
- down_weight_gradient: float32 [2, 3072, 768], P(None, ('row', 'tok'))
- down_bias_gradient: float32 [2, 768], P(None, ('row', 'tok'))
Inputs may be any that keep to these rules, and one draw needn't show every extreme that they name: `valid`: in every row the ones come first and the zeros, at most 64 of them, fill its end.
All inputs are finite; a program needn't handle non-finite values.
Results may differ from a plain program's by a relative error of at most 0.014.
Values may be sent and summed in bfloat16 or wider, within the bound.
No kernel may reach another device: no remote copies, remote signals or barrier semaphores. Data moves between devices by JAX's collectives and lax.ppermute only.
A program may use at most 320 MiB of HBM per device.

v0:
```python
import functools
import math

import jax
import jax.numpy as jnp
from jax import lax
from jax.experimental import pallas as pl
from jax.experimental.pallas import tpu as pltpu
from jax.sharding import PartitionSpec as P

epsilon = 1e-05
score_scale = 0.125
masked_score = -1e30
head_size = 64
lanes = 128
plan = {"F2": (), "jd": (), "u0": (), "B1b": (0,), "B2": (1,), "j0": (0, 2), "tail": (), "first": 1, "orders": "zzzrr", "done": 2}
forward_unroll = 1
backward_unroll = 1
mlp_unroll = 1
f32 = jnp.float32
bf16 = jnp.bfloat16
VMEM = pl.BlockSpec(memory_space=pltpu.VMEM)
SMEM = pl.BlockSpec(memory_space=pltpu.SMEM)
HBM = pl.BlockSpec(memory_space=pltpu.HBM)
ANY = pl.BlockSpec(memory_space=pl.ANY)


def shape(dims, kind):
    return jax.ShapeDtypeStruct(dims, kind)


def dot(left, right):
    return jnp.dot(left, right, preferred_element_type=f32)


def dot_nt(left, right):
    return lax.dot_general(left, right, (((1,), (1,)), ((), ())), preferred_element_type=f32)


def dot_tn(left, right):
    return lax.dot_general(left, right, (((0,), (0,)), ((), ())), preferred_element_type=f32)


def normalize(stream):
    centre = stream - jnp.mean(stream, axis=-1, keepdims=True)
    inverse = lax.rsqrt(jnp.mean(centre * centre, axis=-1, keepdims=True) + epsilon)
    return centre * inverse, inverse


def norm_back(upstream, unit, inverse, gain):
    scaled = upstream * gain
    return inverse * (
        scaled
        - jnp.mean(scaled, axis=-1, keepdims=True)
        - unit * jnp.mean(scaled * unit, axis=-1, keepdims=True)
    )


def column_sum(array):
    return jnp.sum(array, axis=0, keepdims=True)


def gelu_and_slope(x):
    size = jnp.abs(x)
    t = 1.0 / (1.0 + (0.3275911 * 0.7071067811865476) * size)
    bell = jnp.exp(-0.5 * (x * x))
    series = t * (
        0.5 * 0.254829592
        + t
        * (
            0.5 * -0.284496736
            + t * (0.5 * 1.421413741 + t * (0.5 * -1.453152027 + t * (0.5 * 1.061405429)))
        )
    )
    tail = series * bell
    share = jnp.where(x >= 0, 1.0 - tail, tail)
    return x * share, share + x * (bell * 0.3989422804014327)


class Copies:
    def __init__(self, sems):
        self.sems = sems
        self.used = 0
        self.out = []

    def bring(self, source, target):
        copy = pltpu.make_async_copy(source, target, self.sems.at[self.used])
        self.used += 1
        copy.start()
        return copy

    def send(self, source, target):
        self.out.append(self.bring(source, target))

    def thirds(self, source, target, order):
        third = target.shape[1] // 3
        windows = [pl.ds(index * third, third) for index in order]
        return [self.bring(source.at[:, window], target.at[:, window]) for window in windows]

    def finish(self):
        for copy in self.out:
            copy.wait()


def emit_project(stream, layer, gain, shift, bias, weight, waits, normed_ref, query_ref, kv_ref):
    width = stream.shape[1]
    unit, _ = normalize(stream)
    normed_ref[...] = (unit * gain[layer : layer + 1] + shift[layer : layer + 1]).astype(bf16)
    normed = normed_ref[...]
    waits[0].wait()
    kv_ref[:, :width] = dot(normed, weight[:, width : 2 * width]).astype(bf16)
    waits[1].wait()
    kv_ref[:, width:] = (
        dot(normed, weight[:, 2 * width :]) + bias[layer, 1:2]
    ).astype(bf16)
    waits[2].wait()
    queries = (dot(normed, weight[:, :width]) + bias[layer, 0:1]).astype(bf16)
    query_ref[...] = queries * jnp.asarray(score_scale, bf16)


def head_masks():
    lane = lax.broadcasted_iota(jnp.int32, (1, lanes), 1)
    return (lane < head_size, lane >= head_size)


def emit_mask(rows, code_ref, far_ref, mask_ref):
    own = code_ref[...].astype(f32)
    diagonal = lax.broadcasted_iota(jnp.int32, (rows, rows), 0) == lax.broadcasted_iota(
        jnp.int32, (rows, rows), 1
    )
    column = jnp.sum(jnp.where(diagonal, own, 0.0), axis=1, keepdims=True)
    mask_ref[:, :rows] = jnp.where(column == own, 0.0, masked_score)
    mask_ref[:, rows:] = jnp.where(column == far_ref[...].astype(f32), 0.0, masked_score)


def emit_attention(width, query_ref, kv_ref, mask_ref, attended_ref, soft_ref):
    rows = query_ref.shape[0]
    masks = head_masks()
    zero = jnp.zeros((), bf16)

    def one_pair(pair, carry):
        columns = pl.ds(pl.multiple_of(pair * lanes, lanes), lanes)
        value_columns = pl.ds(pl.multiple_of(width + pair * lanes, lanes), lanes)
        queries = query_ref[:, columns]
        both = jnp.concatenate([jnp.where(mask, queries, zero) for mask in masks], axis=0)
        scores = dot_nt(both, kv_ref[:, columns])
        softs = []
        for side in range(2):
            own = scores[side * rows : (side + 1) * rows] + mask_ref[...]
            exponent = jnp.exp(own - jnp.max(own, axis=-1, keepdims=True))
            soft = exponent * (1.0 / jnp.sum(exponent, axis=-1, keepdims=True))
            softs.append(soft.astype(bf16))
            soft_ref[pair * 2 + side] = softs[-1]
        total = dot(jnp.concatenate(softs, axis=0), kv_ref[:, value_columns])
        attended_ref[:, columns] = jnp.where(masks[0], total[:rows], total[rows:]).astype(bf16)
        return carry

    lax.fori_loop(0, width // lanes, one_pair, 0, unroll=forward_unroll)


def emit_attention_back(
    width, query_ref, kv_ref, soft_ref, wait_soft, grad_ref, dq_ref, dq_sum, own_ref, sent_ref
):
    rows = query_ref.shape[0]
    masks = head_masks()
    zero = jnp.zeros((), bf16)
    def one_pair(pair, carry):
        wait_soft(pair)
        columns = pl.ds(pl.multiple_of(pair * lanes, lanes), lanes)
        value_columns = pl.ds(pl.multiple_of(width + pair * lanes, lanes), lanes)
        queries = query_ref[:, columns]
        grads = grad_ref[:, columns]
        keys = kv_ref[:, columns]
        own_grads = [jnp.where(mask, grads, zero) for mask in masks]
        soft_grads = dot_nt(jnp.concatenate(own_grads, axis=0), kv_ref[:, value_columns])
        dq = jnp.zeros((rows, lanes), f32)
        dk = jnp.zeros((2 * rows, lanes), f32)
        dv = jnp.zeros((2 * rows, lanes), f32)
        for side in range(2):
            soft_low = soft_ref[pair * 2 + side]
            soft = soft_low.astype(f32)
            soft_grad = soft_grads[side * rows : (side + 1) * rows]
            delta = jnp.sum(soft_grad * soft, axis=-1, keepdims=True)
            score_grad = (soft * (soft_grad - delta)).astype(bf16)
            dq += dot(score_grad, jnp.where(masks[side], keys, zero))
            dk += dot_tn(score_grad, jnp.where(masks[side], queries, zero))
            dv += dot_tn(soft_low, own_grads[side])
        dq = dq * score_scale
        dq_ref[:, columns] = dq.astype(bf16)
        dq_sum[0:1, columns] = column_sum(dq)
        own_ref[:, columns] = dk[:rows]
        own_ref[:, value_columns] = dv[:rows]
        sent_ref[:, columns] = dk[rows:].astype(bf16)
        sent_ref[:, value_columns] = dv[rows:].astype(bf16)
        return carry

    lax.fori_loop(0, width // lanes, one_pair, 0, unroll=backward_unroll)


def project_kernel(
    gain, shift, bias, tokens_hbm, weight_hbm, grad_hbm,
    query_hbm, packed_hbm, kept_hbm,
    tokens, weight, grad, normed, query, kv, sems,
):
    copies = Copies(sems)
    width = tokens.shape[1]
    half = width // 2
    first = copies.bring(tokens_hbm, tokens)
    third = copies.bring(grad_hbm, grad)
    thirds = copies.thirds(weight_hbm.at[0], weight, (1, 2, 0))
    core = lax.axis_index("tok")
    first.wait()
    third.wait()
    copies.send(
        grad.at[:, pl.ds(pl.multiple_of((1 - core) * half, half), half)],
        packed_hbm.at[:, pl.ds(3 * width, half)],
    )
    copies.send(grad.at[:, pl.ds(pl.multiple_of(core * half, half), half)], kept_hbm)
    emit_project(tokens[...].astype(f32), 0, gain, shift, bias, weight, thirds, normed, query, kv)
    copies.send(kv, packed_hbm.at[:, pl.ds(0, 2 * width)])
    copies.send(normed, packed_hbm.at[:, pl.ds(2 * width, width)])
    copies.send(query, query_hbm)
    copies.finish()


def emit_upper_half(layer, stream, output_weight, bias, gain, shift, acts, middle_ref):
    width = stream.shape[1]
    middle = stream + dot(acts[:, :width], output_weight[...]) + bias[layer : layer + 1]
    middle_ref[...] = middle
    unit, _ = normalize(middle)
    acts[:, width:] = (unit * gain[layer : layer + 1] + shift[layer : layer + 1]).astype(bf16)


def middle_kernel(
    layer, code, code_far, output_bias, gain, shift, up_bias,
    down_bias, next_gain, next_shift, joint_bias,
    stream_hbm, query_hbm, packed_hbm, far_hbm, output_hbm, up_hbm, down_hbm, joint_hbm,
    acts_hbm, hidden_hbm, soft_hbm, middle_hbm, slope_hbm,
    stream_next_hbm, query_next_hbm, packed_next_hbm,
    stream_ref, query, kv, mask, acts, hidden_ref, soft, middle_ref, slope,
    output_weight, up_weight, down_weight, joint_weight, total, normed, query_next, kv_next, sems,
):
    copies = Copies(sems)
    rows, width = query.shape
    inner = up_weight.shape[1]
    kv_window = pl.ds(0, 2 * width)
    wait = [
        copies.bring(query_hbm, query),
        copies.bring(packed_hbm.at[:, kv_window], kv.at[pl.ds(0, rows)]),
        copies.bring(far_hbm.at[:, kv_window], kv.at[pl.ds(rows, rows)]),
        copies.bring(stream_hbm, stream_ref),
    ]
    emit_mask(rows, code, code_far, mask)
    for copy in wait[:3]:
        copy.wait()
    output_copy = copies.bring(output_hbm.at[layer], output_weight)
    up_copy = copies.bring(up_hbm.at[layer], up_weight)
    down_copy = copies.bring(down_hbm.at[layer], down_weight)
    thirds = copies.thirds(joint_hbm.at[layer + 1], joint_weight, (1, 2, 0))
    emit_attention(width, query, kv, mask, acts, soft)
    copies.send(soft, soft_hbm)
    wait[3].wait()
    output_copy.wait()
    emit_upper_half(
        layer,
        stream_ref[...].astype(f32),
        output_weight,
        output_bias,
        gain,
        shift,
        acts,
        middle_ref,
    )
    copies.send(acts, acts_hbm)
    copies.send(middle_ref, middle_hbm)
    up_copy.wait()
    down_copy.wait()
    total[...] = middle_ref[...] + down_bias[layer : layer + 1]
    chunk = width

    def one_chunk(index, carry):
        columns = pl.ds(pl.multiple_of(index * chunk, chunk), chunk)
        preact = dot(acts[:, width:], up_weight[:, columns])
        hidden, rate = gelu_and_slope(preact + up_bias[layer : layer + 1, columns])
        hidden_ref[:, columns] = hidden.astype(bf16)
        slope[:, columns] = rate.astype(bf16)
        total[...] += dot(hidden_ref[:, columns], down_weight[columns, :])
        return carry

    lax.fori_loop(0, inner // chunk, one_chunk, 0, unroll=mlp_unroll)
    copies.send(hidden_ref, hidden_hbm)
    copies.send(slope, slope_hbm)
    copies.send(total, stream_next_hbm)
    emit_project(
        total[...],
        layer + 1,
        next_gain,
        next_shift,
        joint_bias,
        joint_weight,
        thirds,
        normed,
        query_next,
        kv_next,
    )
    copies.send(kv_next, packed_next_hbm.at[:, kv_window])
    copies.send(normed, packed_next_hbm.at[:, pl.ds(2 * width, width)])
    copies.send(query_next, query_next_hbm)
    copies.finish()


def emit_middle_grad(layer, core, upstream, middle, total, gain, vectors, low, grad_ref, grads):
    width = middle.shape[1]
    columns = width // 2
    unit, inverse = normalize(middle)
    normed_grad = total[...]
    vectors[5:6] = column_sum(normed_grad * unit)
    vectors[6:7] = column_sum(normed_grad)
    middle_grad = upstream + norm_back(normed_grad, unit, inverse, gain[layer : layer + 1])
    vectors[4:5] = column_sum(middle_grad)
    grad_ref[...] = middle_grad
    low[...] = middle_grad.astype(bf16)
    behind = grads.shape[2] - columns
    for turn, side in enumerate((1 - core, core)):
        grads[turn, :, behind:] = low[:, pl.ds(pl.multiple_of(side * columns, lanes), columns)]


def turn_kernel(
    layer, code, code_far, output_bias, gain, shift, up_bias, down_bias,
    stream_hbm, query_hbm, packed_hbm, far_hbm, upstream_hbm, output_hbm, up_hbm, down_hbm,
    acts_hbm, hidden_hbm, soft_hbm, result_hbm, kept_hbm, sent_hbm, low_hbm, grad_hbm,
    vectors, up_sum,
    stream_ref, query, kv, mask, acts, hidden_ref, soft, middle_ref, upstream_ref,
    grads, low, grad_ref, result, result_low, total,
    output_weight, up_weight, down_weight, sems,
):
    copies = Copies(sems)
    rows, width = query.shape
    inner = up_weight.shape[1]
    core = lax.axis_index("tok")
    kv_window = pl.ds(0, 2 * width)
    wait = [
        copies.bring(query_hbm, query),
        copies.bring(packed_hbm.at[:, kv_window], kv.at[pl.ds(0, rows)]),
        copies.bring(far_hbm.at[:, kv_window], kv.at[pl.ds(rows, rows)]),
        copies.bring(stream_hbm, stream_ref),
    ]
    emit_mask(rows, code, code_far, mask)
    for copy in wait[:3]:
        copy.wait()
    output_copy = copies.bring(output_hbm.at[layer], output_weight)
    upstream_copy = copies.bring(upstream_hbm, upstream_ref)
    up_copy = copies.bring(up_hbm.at[layer], up_weight)
    down_copy = copies.bring(down_hbm.at[layer], down_weight)
    emit_attention(width, query, kv, mask, acts, soft)
    copies.send(soft, soft_hbm)
    wait[3].wait()
    output_copy.wait()
    emit_upper_half(
        layer,
        stream_ref[...].astype(f32),
        output_weight,
        output_bias,
        gain,
        shift,
        acts,
        middle_ref,
    )
    copies.send(acts, acts_hbm)
    upstream_copy.wait()
    upstream = upstream_ref[...].astype(f32)
    low[...] = upstream.astype(bf16)
    vectors[0:4] = jnp.zeros_like(vectors[0:4])
    vectors[7:8] = column_sum(upstream)
    up_sum[...] = jnp.zeros_like(up_sum)
    result[...] = middle_ref[...] + down_bias[layer : layer + 1]
    total[...] = jnp.zeros_like(total)
    up_copy.wait()
    down_copy.wait()
    chunk = width
    half = inner // 2

    def one_chunk(index, carry):
        turn = index // (half // chunk)
        at = pl.multiple_of(index % (half // chunk) * chunk, chunk)
        side = jnp.where(turn == 0, 1 - core, core)
        columns = pl.ds(pl.multiple_of(side * half + at, chunk), chunk)
        preact = dot(acts[:, width:], up_weight[:, columns])
        hidden, rate = gelu_and_slope(preact + up_bias[layer : layer + 1, columns])
        hidden_ref[:, columns] = hidden.astype(bf16)
        result[...] += dot(hidden_ref[:, columns], down_weight[columns, :])
        preact_grad = dot_nt(low[...], down_weight[columns, :]) * rate
        up_sum[0:1, columns] = column_sum(preact_grad)
        grads[turn, :, pl.ds(at, chunk)] = preact_grad.astype(bf16)
        total[...] += dot_nt(preact_grad.astype(bf16), up_weight[:, columns])
        return carry

    lax.fori_loop(0, inner // chunk, one_chunk, 0, unroll=mlp_unroll)
    copies.send(hidden_ref, hidden_hbm)
    result_low[...] = result[...].astype(bf16)
    copies.send(result_low, result_hbm)
    emit_middle_grad(
        layer,
        core,
        upstream_ref[...].astype(f32),
        middle_ref[...],
        total,
        gain,
        vectors,
        low,
        grad_ref,
        grads,
    )
    copies.send(low, low_hbm)
    copies.send(grads.at[0], sent_hbm)
    copies.send(grads.at[1], kept_hbm)
    copies.send(grad_ref, grad_hbm)
    copies.finish()


def attention_back_kernel(
    layer, low_hbm, query_hbm, packed_hbm, far_hbm, soft_hbm, output_hbm,
    dq_hbm, own_hbm, sent_hbm, dq_sum,
    low, query, kv, soft, attended_grad, output_weight, dq, own, sent, soft_sems, sems,
):
    copies = Copies(sems)
    rows, width = low.shape
    kv_window = pl.ds(0, 2 * width)
    wait = [
        copies.bring(low_hbm, low),
        copies.bring(output_hbm.at[layer], output_weight),
        copies.bring(query_hbm, query),
        copies.bring(packed_hbm.at[:, kv_window], kv.at[pl.ds(0, rows)]),
        copies.bring(far_hbm.at[:, kv_window], kv.at[pl.ds(rows, rows)]),
    ]

    def soft_copy(pair):
        two = pl.ds(pair * 2, 2)
        return pltpu.make_async_copy(soft_hbm.at[two], soft.at[two], soft_sems.at[pair])

    for pair in range(width // lanes):
        soft_copy(pair).start()
    dq_sum[...] = jnp.zeros_like(dq_sum)
    wait[0].wait()
    wait[1].wait()
    attended_grad[...] = dot_nt(low[...], output_weight[...]).astype(bf16)
    for copy in wait[2:]:
        copy.wait()
    emit_attention_back(
        width,
        query,
        kv,
        soft,
        lambda pair: soft_copy(pair).wait(),
        attended_grad,
        dq,
        dq_sum,
        own,
        sent,
    )
    copies.send(sent, sent_hbm)
    copies.send(dq, dq_hbm)
    copies.send(own, own_hbm)
    copies.finish()


def emit_project_back(
    layer, copies, core, wait, thirds, dq_sum, vectors_two, gain, mixed, own, received,
    stream_ref, grad_ref, joint_weight, kept_hbm, sent_hbm, vectors,
):
    rows, width = stream_ref.shape
    wide = 3 * width // 2
    vectors[4:8] = vectors_two[4:8]
    vectors[2:3] = dq_sum[0:1]
    for copy in wait[:3]:
        copy.wait()
    kv_grad = own[...] + received[...].astype(f32)
    mixed[:, width:] = kv_grad.astype(bf16)
    vectors[3:4] = column_sum(kv_grad[:, width:])
    for side, target in ((1 - core, sent_hbm), (core, kept_hbm)):
        copies.send(mixed.at[:, pl.ds(pl.multiple_of(side * wide, lanes), wide)], target)
    normed_grad = jnp.zeros((rows, width), f32)
    for index, copy in enumerate(thirds):
        copy.wait()
        window = slice(index * width, (index + 1) * width)
        normed_grad += dot_nt(mixed[:, window], joint_weight[:, window])
    wait[3].wait()
    unit, inverse = normalize(stream_ref[...].astype(f32))
    vectors[0:1] = column_sum(normed_grad * unit)
    vectors[1:2] = column_sum(normed_grad)
    wait[4].wait()
    return grad_ref[...] + norm_back(normed_grad, unit, inverse, gain[layer : layer + 1])


def project_back_kernel(
    layer, gate, gain, dq_sum, vectors_two,
    dq_hbm, own_hbm, received_hbm, stream_hbm, grad_hbm, joint_hbm,
    kept_hbm, sent_hbm, upstream_hbm, vectors,
    own, received, stream_ref, grad_ref, mixed, upstream, joint_weight, sems,
):
    copies = Copies(sems)
    width = stream_ref.shape[1]
    wait = [
        copies.bring(dq_hbm, mixed.at[:, pl.ds(0, width)]),
        copies.bring(own_hbm, own),
        copies.bring(received_hbm, received),
        copies.bring(stream_hbm, stream_ref),
        copies.bring(grad_hbm, grad_ref),
    ]
    thirds = copies.thirds(joint_hbm.at[layer], joint_weight, (0, 1, 2))
    upstream[...] = emit_project_back(
        layer, copies, lax.axis_index("tok"), wait, thirds, dq_sum, vectors_two, gain, mixed,
        own, received, stream_ref, grad_ref, joint_weight, kept_hbm, sent_hbm, vectors,
    )
    copies.send(upstream, upstream_hbm)
    copies.finish()


def between_kernel(
    above, gate, gain, second_gain, dq_sum, vectors_two,
    dq_hbm, own_hbm, received_hbm, stream_hbm, grad_hbm, slope_hbm, middle_hbm,
    joint_hbm, down_hbm, up_hbm,
    mix_kept_hbm, mix_sent_hbm, up_kept_hbm, up_sent_hbm, kept_hbm, sent_hbm, low_hbm,
    grad_next_hbm, vectors, vectors_next, up_sum,
    own, received, stream_ref, grad_ref, mixed, upstream, low, slope, middle_ref,
    grads, low_next, grad_next, total, joint_weight, down_weight, up_weight, weight_sems, sems,
):
    copies = Copies(sems)
    rows, width = stream_ref.shape
    inner = up_weight.shape[1]
    layer = above - 1
    core = lax.axis_index("tok")
    wait = [
        copies.bring(dq_hbm, mixed.at[:, pl.ds(0, width)]),
        copies.bring(own_hbm, own),
        copies.bring(received_hbm, received),
        copies.bring(stream_hbm, stream_ref),
        copies.bring(grad_hbm, grad_ref),
    ]
    thirds = copies.thirds(joint_hbm.at[above], joint_weight, (0, 1, 2))
    chunk = width
    half = inner // 2

    def window_of(index):
        turn = index // (half // chunk)
        at = pl.multiple_of(index % (half // chunk) * chunk, chunk)
        side = jnp.where(turn == 0, 1 - core, core)
        return turn, at, pl.ds(pl.multiple_of(side * half + at, chunk), chunk)

    def weight_copies(index):
        window = window_of(index)[2]
        return (
            pltpu.make_async_copy(
                down_hbm.at[layer, window], down_weight.at[window], weight_sems.at[0, index]
            ),
            pltpu.make_async_copy(
                up_hbm.at[layer, :, window], up_weight.at[:, window], weight_sems.at[1, index]
            ),
        )

    slope_copy = copies.bring(slope_hbm, slope)
    for index in range(inner // chunk):
        for copy in weight_copies(index):
            copy.start()
    middle_copy = copies.bring(middle_hbm, middle_ref)
    below = emit_project_back(
        above, copies, core, wait, thirds, dq_sum, vectors_two, gain, mixed,
        own, received, stream_ref, grad_ref, joint_weight, mix_kept_hbm, mix_sent_hbm, vectors,
    )
    upstream[...] = below
    low[...] = below.astype(bf16)
    columns = width // 2
    for side, target in ((1 - core, up_sent_hbm), (core, up_kept_hbm)):
        copies.send(low.at[:, pl.ds(pl.multiple_of(side * columns, lanes), columns)], target)
    vectors_next[0:4] = jnp.zeros_like(vectors_next[0:4])
    vectors_next[7:8] = column_sum(below)
    up_sum[...] = jnp.zeros_like(up_sum)
    total[...] = jnp.zeros_like(total)
    slope_copy.wait()

    def one_chunk(index, carry):
        turn, at, window = window_of(index)
        for copy in weight_copies(index):
            copy.wait()
        preact_grad = dot_nt(low[...], down_weight[window, :]) * slope[:, window].astype(f32)
        up_sum[0:1, window] = column_sum(preact_grad)
        grads[turn, :, pl.ds(at, chunk)] = preact_grad.astype(bf16)
        total[...] += dot_nt(preact_grad.astype(bf16), up_weight[:, window])
        return carry

    lax.fori_loop(0, inner // chunk, one_chunk, 0, unroll=mlp_unroll)
    middle_copy.wait()
    emit_middle_grad(
        layer,
        core,
        upstream[...],
        middle_ref[...],
        total,
        second_gain,
        vectors_next,
        low_next,
        grad_next,
        grads,
    )
    copies.send(low_next, low_hbm)
    copies.send(grads.at[0], sent_hbm)
    copies.send(grads.at[1], kept_hbm)
    copies.send(grad_next, grad_next_hbm)
    copies.finish()


def weight_kernel(chips, order, plan, vector_row, *refs):
    core, me = lax.axis_index("tok"), lax.axis_index("row")
    refs = refs[1:]
    if vector_row:
        vectors, up_sum = refs[:2]
        refs = refs[2:]
    count = 1 + max(max(item[0], item[1], item[5], item[6]) for item in plan)
    arrays = refs[:count]
    kept_hbm, sent_hbm = refs[count : count + 2]
    refs = refs[count + 2 :]
    lefts, rights = refs[: len(plan)], refs[len(plan) : 2 * len(plan)]
    block, slot_sems, sems = refs[2 * len(plan) :]
    copies = Copies(sems)
    columns = block.shape[2]
    half = chips // 2
    steps = chips.bit_length() - 1
    waits = []
    for item, left, right in zip(plan, lefts, rights):
        own, far, at, at_far, size, right_own, right_far, right_at, right_at_far, strips, row = item
        piece = min(size, 768)
        wait = []
        for first in range(0, size, piece):
            for side, array, start in ((0, own, at), (1, far, at_far)):
                wait.append(
                    copies.bring(
                        arrays[array].at[:, pl.ds(start + first, piece)],
                        left.at[side, :, pl.ds(first, piece)],
                    )
                )
        for side, array, start in ((0, right_own, right_at), (1, right_far, right_at_far)):
            window = pl.ds(start, strips * columns)
            wait.append(copies.bring(arrays[array].at[:, window], right.at[side]))
        waits.append(wait)
    slots = []
    for chip in range(chips):
        apart = chip ^ me
        slot = 0
        for step in range(steps):
            bit = jnp.where(core == 0, step_bit(order, step, 0), step_bit(order, step, 1))
            slot = slot * 2 + ((apart >> bit) & 1)
        slots.append(slot)
    outgoing = []

    def send_rows(chip, row, count):
        sem = slot_sems.at[len(outgoing)]
        window = pl.ds(row, count)
        source = block.at[slots[chip], window]

        @pl.when(slots[chip] >= half)
        def _():
            target = sent_hbm.at[slots[chip] - half, window]
            pltpu.make_async_copy(source, target, sem).start()

        @pl.when(slots[chip] < half)
        def _():
            pltpu.make_async_copy(source, kept_hbm.at[slots[chip], window], sem).start()

        outgoing.append(pltpu.make_async_copy(source, kept_hbm.at[0, window], sem))

    if vector_row:
        depth = 16
        width, inner = vectors.shape[1], up_sum.shape[1]

        def one_slot(slot, carry):
            apart = sum(
                ((slot >> (steps - 1 - step)) & 1)
                << jnp.where(core == 0, step_bit(order, step, 0), step_bit(order, step, 1))
                for step in range(steps)
            )
            chip = me ^ apart
            short = pltpu.roll(vectors[...], width - chip * (width // chips), axis=1)
            wide = pltpu.roll(up_sum[...], inner - chip * (inner // chips), axis=1)
            block[slot, vector_row : vector_row + depth, :] = jnp.concatenate(
                [short[:, :columns], wide[:, :columns]], axis=0
            ).astype(bf16)
            return carry

        lax.fori_loop(0, chips, one_slot, 0)
    for item, left, right, wait in zip(plan, lefts, rights, waits):
        size, strips, row = item[4], item[9], item[10]
        part = size // chips
        piece = min(size, 768)
        for first in range(0, size, piece):
            flipped = []
            for side in range(2):
                wait[first // piece * 2 + side].wait()
                flipped.append(left[side, :, first : first + piece].T)
            if not first:
                wait[-2].wait()
                wait[-1].wait()
            for strip in range(strips):
                window = slice(strip * columns, (strip + 1) * columns)
                product = dot(flipped[0], right[0, :, window]) + dot(
                    flipped[1], right[1, :, window]
                )
                product = product.astype(bf16)
                for cut in range(0, piece, part):
                    slot = slots[(first + cut) // part]
                    block[slot, row + strip * part : row + (strip + 1) * part, :] = product[
                        cut : cut + part
                    ]
            for cut in range(0, piece, part):
                with_them = vector_row == row + strips * part
                send_rows(
                    (first + cut) // part, row, strips * part + (depth if with_them else 0)
                )
    for copy in outgoing:
        copy.wait()


def sum_kernel(groups, *refs):
    count = len(groups)
    steps = (len(refs) - 2 - count - 4) // count
    inputs = refs[: count * steps]
    kept_hbm, sent_hbm = refs[count * steps : 2 + count * steps]
    buffers = refs[2 + count * steps : 2 + count * steps + count]
    total, kept, sent, sems = refs[2 + count * steps + count :]
    copies = Copies(sems)
    core = lax.axis_index("tok")
    waits = [
        [
            copies.bring(inputs[g * steps + step].at[0], buffers[g].at[step])
            for step in range(steps)
        ]
        for g in range(count)
    ]
    out = 0
    for g, pieces in enumerate(groups):
        for copy in waits[g]:
            copy.wait()
        rows = buffers[g].shape[1]
        value = buffers[g][0].astype(f32)
        for step in range(1, steps):
            value += buffers[g][step].astype(f32)
        total[:rows] = value
        for row, part, repeats in pieces:
            if not repeats:
                kept[out : out + part] = total[row : row + part]
                sent[out : out + part] = total[row : row + part]
                out += part
            for repeat in range(repeats):
                first = row + repeat * 2 * part
                kept[out : out + part] = total[pl.ds(pl.multiple_of(first + core * part, 8), part)]
                sent[out : out + part] = total[
                    pl.ds(pl.multiple_of(first + (1 - core) * part, 8), part)
                ]
                out += part
    copies.send(sent, sent_hbm)
    copies.send(kept, kept_hbm)
    copies.finish()


def place_kernel(places, *refs):
    count = len(places)
    inputs, outputs = refs[: 2 * count], refs[2 * count : -2 * count - 1]
    buffers, sems = refs[-2 * count - 1 : -1], refs[-1]
    copies = Copies(sems)
    wait = [copies.bring(source, target) for source, target in zip(inputs, buffers)]
    core = lax.axis_index("tok")
    for number, group in enumerate(places):
        kept, far = buffers[2 * number : 2 * number + 2]
        columns = kept.shape[1]
        for copy in wait[2 * number : 2 * number + 2]:
            copy.wait()
        for place in group:
            if len(place) == 5:
                first, part, index, layer, strips = place
                for strip in range(strips):
                    rows = slice(first + strip * part, first + (strip + 1) * part)
                    for side, source in ((core, kept), (1 - core, far)):
                        at = pl.multiple_of(side * (strips * columns) + strip * columns, lanes)
                        outputs[index][layer, :, pl.ds(at, columns)] = source[rows, :]
            else:
                first, half, layer = place
                short = kept[first : first + half] + far[first : first + half]
                wide = kept[first + half : first + 2 * half] + far[first + half : first + 2 * half]
                size, wide_size = outputs[4].shape[1], outputs[11].shape[1]
                short = pltpu.roll(short, columns - core * size, axis=1)
                wide = pltpu.roll(wide, columns - core * wide_size, axis=1)
                outputs[4][layer : layer + 1] = short[0:1, :size]
                outputs[5][layer : layer + 1] = short[1:2, :size]
                outputs[6][layer] = short[2:4, :size]
                for row, index in ((4, 7), (5, 8), (6, 9), (7, 10)):
                    outputs[index][layer : layer + 1] = short[row : row + 1, :size]
                outputs[11][layer : layer + 1] = wide[0:1, :wide_size]


def call(kernel, outs, ins, scratch, *arrays, flops=0, out_specs=None, limit=58):
    out_specs = tuple(out_specs or (ANY for _ in outs))
    count = sum(math.prod(a.shape) * a.dtype.itemsize for a in list(arrays) + list(outs))
    held = [kept for kept in scratch if kept.memory_space == pltpu.VMEM]
    held += [a for a, spec in zip(list(arrays) + list(outs), list(ins) + list(out_specs)) if spec is VMEM]
    need = sum(math.prod(a.shape) * a.dtype.itemsize for a in held) + (8 << 20)
    return pl.pallas_call(
        kernel,
        out_shape=tuple(outs),
        in_specs=list(ins),
        out_specs=out_specs,
        scratch_shapes=scratch,
        compiler_params=pltpu.CompilerParams(vmem_limit_bytes=max(need, limit << 20)),
        cost_estimate=pl.CostEstimate(flops=flops, bytes_accessed=count, transcendentals=0),
    )(*arrays)


def swap_cores(array):
    return lax.ppermute(array, "tok", [(0, 1), (1, 0)])


def after(array, *others):
    return lax.optimization_barrier((array,) + others)[0]


def step_bit(order, step, core):
    bit = order[step] if step < len(order) else step
    return bit ^ core if bit < 2 else bit


def distance(chips, order, slot, core):
    steps = chips.bit_length() - 1
    bits = [step_bit(order, step, core) for step in range(steps) if slot >> (steps - 1 - step) & 1]
    return sum(1 << bit for bit in bits)


def step_pairs(chips, order, step):
    return [
        (chip * 2 + core, (chip ^ (1 << step_bit(order, step, core))) * 2 + core)
        for chip in range(chips)
        for core in range(2)
    ]


class Halving:
    def __init__(self, kept, sent, chips, order=(0, 1)):
        self.chips = chips
        self.order = order
        self.slots = chips // 2
        self.step = 0
        self.parts = [kept]
        self.move(sent)

    def move(self, sent):
        pairs = step_pairs(self.chips, self.order, self.step)
        self.parts.append(lax.ppermute(sent, ("row", "tok"), pairs))
        self.step += 1

    def next(self, before=None):
        half = self.slots // 2
        sent = sum(part[half : self.slots].astype(f32) for part in self.parts)
        sent = sent.astype(self.parts[0].dtype)
        if before is not None:
            sent = after(sent, before)
        self.slots = half
        self.move(sent)
        return sent

    def rest(self):
        while self.slots > 1:
            self.next()
        return self


def slots_of_chips(chips, me, core):
    sides = [[distance(chips, (0, 1), slot, side) for slot in range(chips)] for side in range(2)]
    return me ^ jnp.asarray(sides, jnp.int32)[core]


def plain_sums(left, left_far, right, right_far, slots, chips, core):
    product = dot_tn(
        jnp.concatenate([left, left_far], axis=0), jnp.concatenate([right, right_far], axis=0)
    ).astype(bf16)
    product = product.reshape(chips, -1, product.shape[1])[slots]
    done = Halving(product[: chips // 2], product[chips // 2 :], chips).rest()
    total = sum(part[0].astype(f32) for part in done.parts)
    total = total.reshape(2, -1, total.shape[1])
    kept = lax.dynamic_index_in_dim(total, core, 0, keepdims=False)
    other = swap_cores(lax.dynamic_index_in_dim(total, 1 - core, 0, keepdims=False))
    return jnp.where(
        core == 0,
        jnp.concatenate([kept, other], axis=1),
        jnp.concatenate([other, kept], axis=1),
    )


def plain_vectors(vectors, slots, chips, core):
    pieces = [vector.reshape(chips, 2, -1) for vector in vectors]
    packed = jnp.concatenate(pieces, axis=2)
    sent = lax.dynamic_index_in_dim(packed, 1 - core, 1, keepdims=False)
    packed = lax.dynamic_index_in_dim(packed, core, 1, keepdims=False) + swap_cores(sent)
    packed = packed[slots]
    done = Halving(packed[: chips // 2], packed[chips // 2 :], chips).rest()
    packed = sum(part[0] for part in done.parts)
    cuts, at = [], 0
    for piece in pieces:
        cuts.append(packed[at : at + piece.shape[2]])
        at += piece.shape[2]
    return cuts


def body(
    tokens,
    cotangent,
    segment_ids,
    valid,
    first_gain,
    first_shift,
    joint_weight,
    joint_bias,
    output_weight,
    output_bias,
    second_gain,
    second_shift,
    up_weight,
    up_bias,
    down_weight,
    down_bias,
    chips,
):
    layers, width = joint_weight.shape[:2]
    inner = up_weight.shape[2]
    heads = width // head_size
    rows = tokens.shape[1]
    columns = width // 2
    wide = 3 * columns
    part = width // chips
    native = part % 48 == 0
    strips_up = inner // 2 // columns
    strips_joint = wide // columns
    core = lax.axis_index("tok").astype(jnp.int32)
    code = segment_ids * 2 + valid
    code_far = swap_cores(code)
    dma = pltpu.SemaphoreType.DMA
    weights = (joint_weight, output_weight, up_weight, down_weight)

    def vm(*sizes, kind=bf16):
        return pltpu.VMEM(sizes, kind)

    def low_shape(*sizes):
        return shape(sizes, bf16)

    def full_shape(*sizes):
        return shape(sizes, f32)

    def places_of(arrays):
        return [HBM if any(array is weight for weight in weights) else ANY for array in arrays]

    def wired(kernel, small, large, outs, scratch, flops, vector_outs=0):
        return call(
            kernel,
            outs,
            [VMEM] * len(small) + places_of(large),
            scratch,
            *small,
            *large,
            flops=flops,
            out_specs=[ANY] * (len(outs) - vector_outs) + [VMEM] * vector_outs,
        )

    tokens = tokens[0]
    cotangent = cotangent[0]
    last = layers - 1
    query, packed, up_kept = wired(
        project_kernel,
        [first_gain, first_shift, joint_bias],
        [tokens, joint_weight, cotangent],
        [low_shape(rows, width), low_shape(rows, 3 * width + columns), low_shape(rows, columns)],
        [
            vm(rows, width),
            vm(width, 3 * width),
            vm(rows, width),
            vm(rows, width),
            vm(rows, width),
            vm(rows, 2 * width),
            dma((12,)),
        ],
        2 * rows * width * 3 * width,
    )
    saved = []
    stream = tokens
    for layer in range(last):
        far = swap_cores(packed)
        gate = [item for kept in saved for item in kept[-2:]]
        acts, hidden, soft, middle, slope, stream_next, query_next, packed_next = wired(
            functools.partial(middle_kernel, layer),
            [after(code, *gate), code_far, output_bias, second_gain, second_shift, up_bias]
            + [down_bias, first_gain, first_shift, joint_bias],
            [stream, query, packed, far, output_weight, up_weight, down_weight, joint_weight],
            [
                low_shape(rows, 2 * width),
                low_shape(rows, inner),
                low_shape(heads, rows, 2 * rows),
                full_shape(rows, width),
                low_shape(rows, inner),
                full_shape(rows, width),
                low_shape(rows, width),
                low_shape(rows, 3 * width),
            ],
            [
                vm(rows, width, kind=stream.dtype),
                vm(rows, width),
                vm(2 * rows, 2 * width),
                vm(rows, 2 * rows, kind=f32),
                vm(rows, 2 * width),
                vm(rows, inner),
                vm(heads, rows, 2 * rows),
                vm(rows, width, kind=f32),
                vm(rows, inner),
                vm(width, width),
                vm(width, inner),
                vm(inner, width),
                vm(width, 3 * width),
                vm(rows, width, kind=f32),
                vm(rows, width),
                vm(rows, width),
                vm(rows, 2 * width),
                dma((24,)),
            ],
            2 * rows * width * (2 * inner + 4 * width + 4 * rows),
        )
        saved.append(
            (stream, query, packed, far, acts, hidden, soft, middle, slope)
            + (swap_cores(acts), swap_cores(hidden))
        )
        stream, query, packed = stream_next, query_next, packed_next

    mixed_columns = inner // 2 + columns
    far = swap_cores(packed)
    gate = [item for kept in saved for item in kept[-2:]] if len(saved) > 1 else []
    got = wired(
        functools.partial(turn_kernel, last),
        [after(code, *gate), code_far, output_bias, second_gain, second_shift, up_bias, down_bias],
        [stream, query, packed, far, cotangent, output_weight, up_weight, down_weight],
        [
            low_shape(rows, 2 * width),
            low_shape(rows, inner),
            low_shape(heads, rows, 2 * rows),
            low_shape(rows, width),
            low_shape(rows, mixed_columns),
            low_shape(rows, mixed_columns),
            low_shape(rows, width),
            full_shape(rows, width),
            full_shape(8, width),
            full_shape(8, inner),
        ],
        [
            vm(rows, width, kind=stream.dtype),
            vm(rows, width),
            vm(2 * rows, 2 * width),
            vm(rows, 2 * rows, kind=f32),
            vm(rows, 2 * width),
            vm(rows, inner),
            vm(heads, rows, 2 * rows),
            vm(rows, width, kind=f32),
            vm(rows, width),
            vm(2, rows, mixed_columns),
            vm(rows, width),
            vm(rows, width, kind=f32),
            vm(rows, width, kind=f32),
            vm(rows, width),
            vm(rows, width, kind=f32),
            vm(width, width),
            vm(width, inner),
            vm(inner, width),
            dma((24,)),
        ],
        2 * rows * width * (4 * inner + width + 4 * rows),
        vector_outs=2,
    )
    acts, hidden, soft, output, preact_kept, preact_sent, low, middle_grad = got[:8]
    vectors_two, up_sum = got[8:]
    saved.append(
        (stream, query, packed, far, acts, hidden, soft, None, None)
        + (swap_cores(acts), swap_cores(hidden))
    )

    def attention_back(layer, low, gate):
        query, packed, far, _, _, soft = saved[layer][1:7]
        return wired(
            functools.partial(attention_back_kernel, layer),
            [],
            [after(low, *gate), query, packed, far, soft, output_weight],
            [
                low_shape(rows, width),
                full_shape(rows, 2 * width),
                low_shape(rows, 2 * width),
                full_shape(8, width),
            ],
            [
                vm(rows, width),
                vm(rows, width),
                vm(2 * rows, 2 * width),
                vm(heads, rows, 2 * rows),
                vm(rows, width),
                vm(width, width),
                vm(rows, width),
                vm(rows, 2 * width, kind=f32),
                vm(rows, 2 * width),
                dma((heads // 2,)),
                dma((8,)),
            ],
            2 * rows * width * (width + 10 * rows),
            vector_outs=1,
        )

    back_scratch = [
        vm(rows, 2 * width, kind=f32),
        vm(rows, 2 * width),
        vm(rows, width, kind=f32),
        vm(rows, width, kind=f32),
        vm(rows, 3 * width),
        vm(rows, width, kind=f32),
    ]

    def project_back(layer, dq, own, received, dq_sum, vectors_two, middle_grad, gate):
        stream = saved[layer][0]
        scratch = list(back_scratch)
        scratch[2] = vm(rows, width, kind=stream.dtype)
        return wired(
            functools.partial(project_back_kernel, layer),
            [after(code, *gate), first_gain, dq_sum, vectors_two],
            [dq, own, received, stream, middle_grad, joint_weight],
            [
                low_shape(rows, wide),
                low_shape(rows, wide),
                full_shape(rows, width),
                full_shape(8, width),
            ],
            scratch + [vm(width, 3 * width), dma((16,))],
            2 * rows * width * 3 * width,
            vector_outs=1,
        )

    def between(above, dq, own, received, dq_sum, vectors_two, middle_grad, gate):
        stream = saved[above][0]
        middle, slope = saved[above - 1][7:9]
        return wired(
            functools.partial(between_kernel, above),
            [after(code, *gate), first_gain, second_gain, dq_sum, vectors_two],
            [dq, own, received, stream, middle_grad, slope, middle]
            + [joint_weight, down_weight, up_weight],
            [
                low_shape(rows, wide),
                low_shape(rows, wide),
                low_shape(rows, columns),
                low_shape(rows, columns),
                low_shape(rows, mixed_columns),
                low_shape(rows, mixed_columns),
                low_shape(rows, width),
                full_shape(rows, width),
                full_shape(8, width),
                full_shape(8, width),
                full_shape(8, inner),
            ],
            back_scratch
            + [
                vm(rows, width),
                vm(rows, inner),
                vm(rows, width, kind=f32),
                vm(2, rows, mixed_columns),
                vm(rows, width),
                vm(rows, width, kind=f32),
                vm(rows, width, kind=f32),
                vm(width, 3 * width),
                vm(inner, width),
                vm(width, inner),
                dma((2, inner // width)),
                dma((24,)),
            ],
            2 * rows * width * (3 * width + 2 * inner),
            vector_outs=3,
        )

    groups = []
    gate = []

    def start(order, items, gate_arrays, vectors=()):
        arrays, plan, pieces, places = [], [], [], []
        row, vector_row = 0, 0

        def number(array):
            for index, known in enumerate(arrays):
                if known is array:
                    return index
            arrays.append(array)
            return len(arrays) - 1

        for left, left_far, at, at_far, size, right, right_far, r_at, r_at_far, strips, kind in items:
            left, left_far, right, right_far = map(number, (left, left_far, right, right_far))
            plan.append(
                (left, left_far, at, at_far, size, right, right_far, r_at, r_at_far, strips, row)
            )
            pieces.append((row, size // chips // 2, strips))
            places.append((size // chips // 2, kind[0], kind[1], strips))
            row += strips * size // chips
        if vectors:
            vector_row = row
            pieces.append((row, 16, 0))
            places.append((16, vectors[2]))
            row += 16
        depth = sum(item[9] * item[4] for item in plan)
        kept, sent = call(
            functools.partial(weight_kernel, chips, order, tuple(plan), vector_row),
            (low_shape(chips // 2, row, columns),) * 2,
            [ANY] + [VMEM] * len(vectors[:2]) + [ANY] * len(arrays),
            [vm(2, rows, item[4]) for item in plan]
            + [vm(2, rows, item[9] * columns) for item in plan]
            + [
                vm(chips, row, columns),
                dma((chips * len(plan),)),
                dma((sum(2 * max(1, item[4] // 768) + 2 for item in plan),)),
            ],
            after(code, *gate_arrays),
            *vectors[:2],
            *arrays,
            flops=4 * rows * columns * depth,
        )
        groups.append((Halving(kept, sent, chips, order), row, pieces, places))
        return kept

    def step(*which):
        return [
            groups[index][0].next() if index >= 0 else groups[~index][0].parts[-1]
            for index in which
            if max(index, ~index) < len(groups) and (index < 0 or groups[index][0].slots > 1)
        ]

    orders = [{"z": (0, 2, 1), "r": (0, 1, 2)}[letter] for letter in plan["orders"]]

    def down_item(layer, up_kept, up_far, at_far):
        hidden, hidden_far = saved[layer][5], saved[layer][10]
        return (hidden, hidden_far, 0, 0, inner, up_kept, up_far, 0, at_far, 1, (3, layer))

    def up_items(layer, kept, far):
        acts, acts_far = saved[layer][4], saved[layer][9]
        return [
            (acts, acts_far, width, width, width, kept, far, 0, 0, strips_up, (2, layer)),
            (acts, acts_far, 0, 0, width, kept, far, inner // 2, inner // 2, 1, (1, layer)),
        ]

    def joint_item(layer, kept, far):
        packed, packed_far = saved[layer][2], saved[layer][3]
        at = 2 * width
        return (packed, packed_far, at, at, width, kept, far, 0, 0, strips_joint, (0, layer))

    preact_far = swap_cores(preact_sent)
    dq, own, sent, dq_sum = attention_back(last, low, [])
    received = swap_cores(sent)
    joints = []
    loose = []
    if native:
        items = [down_item(last, up_kept, saved[0][3], 3 * width)]
        if plan["first"]:
            gate = [start(orders[0], items + up_items(last, preact_kept, preact_far), [dq])]
        else:
            gate = [start(orders[0], items, [dq])]
            gate = [start(orders[1], up_items(last, preact_kept, preact_far), gate)]
        gate += step(*plan["F2"])
    else:
        up_far = saved[0][3][:, 3 * width :]
        loose.append((last, up_kept, up_far, preact_kept, preact_far))
    for above in reversed(range(1, layers)):
        layer = above - 1
        got = between(above, dq, own, received, dq_sum, vectors_two, middle_grad, gate)
        mix_kept, mix_sent, up_kept, up_sent, preact_kept, preact_sent, low, middle_grad = got[:8]
        vectors_one, vectors_two, up_sum_next = got[8:]
        mix_far, up_far = swap_cores(mix_sent), swap_cores(up_sent)
        preact_far = swap_cores(preact_sent)
        gate = [low]
        if native:
            items = [joint_item(above, mix_kept, mix_far), down_item(layer, up_kept, up_far, 0)]
            gate += step(*plan["jd"])
            gate = [start(orders[-3], items, gate, (vectors_one, up_sum, above))]
            gate += step(*plan["u0"])
            gate = [start(orders[-2], up_items(layer, preact_kept, preact_far), gate)]
            gate += step(*plan["B1b"])
        else:
            joints.append((above, mix_kept, mix_far, vectors_one, up_sum))
            loose.append((layer, up_kept, up_far, preact_kept, preact_far))
        up_sum = up_sum_next
        dq, own, sent, dq_sum = attention_back(layer, low, gate)
        received = swap_cores(sent)
        gate = [dq] + step(*plan["B2"])
    got = project_back(0, dq, own, received, dq_sum, vectors_two, middle_grad, gate)
    mix_kept, mix_sent, input_gradient, vectors_one = got
    mix_far = swap_cores(mix_sent)
    if native:
        gate = [input_gradient] + step(*plan["j0"])
        kept = start(
            orders[-1], [joint_item(0, mix_kept, mix_far)], gate, (vectors_one, up_sum, 0)
        )
        tail = kept
        for index in plan["tail"]:
            if index < 0:
                tail = after(groups[~index][0].parts[-1], tail)
            elif groups[index][0].slots > 1:
                tail = groups[index][0].next(tail)
    else:
        joints.append((0, mix_kept, mix_far, vectors_one, up_sum))
        return plain_outputs(
            output, input_gradient, saved, loose, joints, chips, core, layers, width, inner
        )

    half = part // 2
    outs = [
        full_shape(layers, half, 3 * width),
        full_shape(layers, half, width),
        full_shape(layers, half, inner),
        full_shape(layers, inner // chips // 2, width),
        full_shape(layers, half),
        full_shape(layers, half),
        full_shape(layers, 2, half),
        full_shape(layers, half),
        full_shape(layers, half),
        full_shape(layers, half),
        full_shape(layers, half),
        full_shape(layers, inner // chips // 2),
    ]

    def finish(some, gate_arrays):
        parts, pieces, places, group_rows, base = [], [], [], [], 0
        for halving, count, group_pieces, group_places in some:
            parts += halving.rest().parts
            pieces.append(tuple(group_pieces))
            group_rows.append(count)
            for place in group_places:
                if len(place) == 4:
                    size, index, layer, strips = place
                    places.append((base, size, index, layer, strips))
                    base += size * strips
                else:
                    places.append((base, 8, place[1]))
                    base += 16
        steps = len(parts) // len(some)
        if gate_arrays:
            parts[0] = after(parts[0], *gate_arrays)
        kept, sent = call(
            functools.partial(sum_kernel, pieces),
            (full_shape(base, columns),) * 2,
            [ANY] * len(parts),
            [vm(steps, count, columns) for count in group_rows]
            + [
                vm(max(group_rows), columns, kind=f32),
                vm(base, columns, kind=f32),
                vm(base, columns, kind=f32),
                dma((len(parts) + 2,)),
            ],
            *parts,
        )
        return kept, swap_cores(sent), places

    split = plan["done"]
    done = [
        finish(some, (tail,) if plan["tail"] else ())
        for some in (groups[:split], groups[split:])
        if some
    ]
    final = call(
        functools.partial(place_kernel, [places for _, _, places in done]),
        outs,
        [ANY] * (2 * len(done)),
        [vm(*array.shape, kind=f32) for kept, far, _ in done for array in (kept, far)]
        + [dma((2 * len(done),))],
        *[array for kept, far, _ in done for array in (kept, far)],
        out_specs=(VMEM,) * len(outs),
    )
    joints, outputs, ups, downs, gain_one, shift_one, biases = final[:7]
    bias_out, gain_two, shift_two, bias_down, bias_up = final[7:]
    return (
        output[None],
        input_gradient[None],
        gain_one,
        shift_one,
        joints,
        biases,
        outputs,
        bias_out,
        gain_two,
        shift_two,
        ups,
        bias_up,
        downs,
        bias_down,
    )


def plain_outputs(
    output, input_gradient, saved, loose, joints, chips, core, layers, width, inner
):
    slots = slots_of_chips(chips, lax.axis_index("row").astype(jnp.int32), core)
    split = functools.partial(plain_sums, slots=slots, chips=chips, core=core)
    mats, vecs = [[None] * 4 for _ in range(layers)], [None] * layers
    for layer, up_kept, up_far, preact_kept, preact_far in loose:
        acts, hidden, acts_far, hidden_far = (saved[layer][index] for index in (4, 5, 9, 10))
        cut = inner // 2
        mats[layer][1] = split(
            acts[:, :width], acts_far[:, :width], preact_kept[:, cut:], preact_far[:, cut:]
        )
        mats[layer][2] = split(
            acts[:, width:], acts_far[:, width:], preact_kept[:, :cut], preact_far[:, :cut]
        )
        mats[layer][3] = split(hidden, hidden_far, up_kept, up_far)
    for layer, mix_kept, mix_far, vectors, up_sum in joints:
        packed, packed_far = saved[layer][2:4]
        window = slice(2 * width, 3 * width)
        mats[layer][0] = split(packed[:, window], packed_far[:, window], mix_kept, mix_far)
        vecs[layer] = [vectors[row] for row in range(8)] + [up_sum[0]]
    cuts = plain_vectors(
        [vector for layer in range(layers) for vector in vecs[layer]], slots, chips, core
    )

    def stacked(position):
        return jnp.stack([cuts[layer * 9 + position] for layer in range(layers)])

    def matrix(position):
        return jnp.stack([mats[layer][position] for layer in range(layers)])

    return (
        output[None],
        input_gradient[None],
        stacked(0),
        stacked(1),
        matrix(0),
        jnp.stack([stacked(2), stacked(3)], axis=1),
        matrix(1),
        stacked(4),
        stacked(5),
        stacked(6),
        matrix(2),
        stacked(8),
        matrix(3),
        stacked(7),
    )


def solution(mesh):
    chips = mesh.shape["row"]
    split = P("row", "tok", None)
    in_specs = (split, split, P("row", "tok"), P("row", "tok")) + (P(),) * 12
    vector = P(None, ("row", "tok"))
    table = P(None, ("row", "tok"), None)
    out_specs = (
        split,
        split,
        vector,
        vector,
        table,
        P(None, None, ("row", "tok")),
        table,
        vector,
        vector,
        vector,
        table,
        vector,
        table,
        vector,
    )

    def run(*arrays):
        return body(*arrays, chips=chips)

    return jax.shard_map(run, mesh=mesh, in_specs=in_specs, out_specs=out_specs, check_vma=False)
```

profile of v0, /device:TPU:0, one launch (start us, length us, event | category | flops | bytes accessed | tf_op | source)
XLA Modules:
  0.0 243.1 jit_solution(16249901157219816705)
XLA Ops:
  0.7 4.8 %shard_map.263 = (bf16[256,768]{1,0:T(8,128)(2,1)}, bf16[256,2688]{1,0:T(8,128)(2,1)}, bf16[256,384]{1,0:T(8,128)(2,1)}) custom-call(f32[2,768]{1,0:T(2,128)} %gain.9, f32[2,768]{1,0:T(2,128)} %next_shift.1, f32[2,2,768]{2,1,0:T(2,128)} %joint_bias.1, bf16[256,768]{1,0:T(8,128)(2,1)} %bitcast.4, bf16[2,768,2304]{2,1,0:T(8,128)(2,1)} %joint_hbm.5, ...), custom_call_target="tpu_custom_call" | custom-call | flops 905969664 | bytes 9854976 | tf_op jit(solution)/shard_map/pallas_call | solution.py:805
  6.1 2.5 %collective-permute-done.code_far = s32[1,256]{1,0:T(1,128)S(1)} collective-permute-done((s32[1,256]{1,0:T(1,128)S(1)}, s32[1,256]{1,0:T(1,128)S(1)}, u32[]{:S(2)}, u32[]{:S(2)}) %collective-permute-start) | collective-permute-done | bytes 1056 | tf_op jit(solution)/shard_map/ppermute | solution.py:817
  10.0 17.7 %shard_map.264 = (bf16[256,1536]{1,0:T(8,128)(2,1)}, bf16[256,3072]{1,0:T(8,128)(2,1)}, bf16[12,256,512]{2,1,0:T(8,128)(2,1)}, f32[256,768]{1,0:T(8,128)}, bf16[...) custom-call(s32[1,256]{1,0:T(1,128)} %copy-done.21, ...), custom_call_target="tpu_custom_call" | custom-call | flops 4026531840 | bytes 42149888 | tf_op jit(solution)/shard_map/pallas_call | solution.py:805
  28.1 2.7 %collective-permute-done.2.far_hbm.refs_4_ = bf16[256,2304]{1,0:T(8,128)(2,1)S(1)} collective-permute-done((bf16[256,2304]{1,0:T(8,128)(2,1)}, bf16[256,2304]{1,0:T(8,128)(2,1)S(1)}, u32[]{:S(2)}, u32[]{:S(2)}) %collective-permute-start.2) | collective-permute-done | bytes 1179680 | tf_op jit(solution)/shard_map/ppermute | solution.py:817
  31.9 20.8 %shard_map.265 = (bf16[256,1536]{1,0:T(8,128)(2,1)}, bf16[256,3072]{1,0:T(8,128)(2,1)}, bf16[12,256,512]{2,1,0:T(8,128)(2,1)}, bf16[256,768]{1,0:T(8,128)(2,1)},...) custom-call(s32[1,256]{1,0:T(1,128)} %copy-done.21, ...), custom_call_target="tpu_custom_call" | custom-call | flops 5536481280 | bytes 34383872 | tf_op jit(solution)/shard_map/pallas_call | solution.py:805
  53.7 10.8 %shard_map.266 = (bf16[256,768]{1,0:T(8,128)(2,1)}, f32[256,1536]{1,0:T(8,128)}, bf16[256,1536]{1,0:T(8,128)(2,1)}, f32[8,768]{1,0:T(8,128)}) custom-call(bf16[256,768]{1,0:T(8,128)(2,1)} %get-tuple-element.95.low_hbm, bf16[256,768]{1,0:T(8,128)(2,1)} %get-tuple-element.92.query_hbm, bf16[256,2304]{1,0:T(8,128)(2,1)} %get-tuple-element.93.packed_hbm.refs_3_, ...), custom_call_target="tpu_custom_call" | custom-call | flops 1308622848 | bytes 11427840 | tf_op jit(solution)/shard_map/pallas_call | solution.py:805
  66.7 9.3 %shard_map.267 = (bf16[8,432,384]{2,1,0:T(8,128)(2,1)}, bf16[8,432,384]{2,1,0:T(8,128)(2,1)}) custom-call(s32[1,256]{1,0:T(1,128)} %copy-done.21, bf16[256,3072]{1,0:T(8,128)(2,1)} %get-tuple-element.99.refs_1_, bf16[256,3072]{1,0:T(8,128)(2,1)} %copy-done.26, bf16[256,384]{1,0:T(8,128)(2,1)} %get-tuple-element.100.refs_3_, bf16[256,2688]{1,0:T(8,128)(2,1)} %copy-done, ...), custom_call_target="tpu_custom_call" | custom-call | flops 2717908992 | bytes 13566976 | tf_op jit(solution)/shard_map/pallas_call | solution.py:805
  76.0 2.7 %collective-permute-start.12 = (bf16[8,432,384]{2,1,0:T(8,128)(2,1)}, bf16[8,432,384]{2,1,0:T(8,128)(2,1)S(1)}, u32[]{:S(2)}, u32[]{:S(2)}) collective-permute-start(bf16[8,432,384]{2,1,0:T(8,128)(2,1)} %get-tuple-element.128), channel_id=1, source_target_pairs={{0,2},{1,5},{2,0},{3,7},{4,6},{5,1},{6,4},{7,3},{8,10},{9,13},{10,... | collective-permute-start | bytes 7962632 | tf_op jit(solution)/shard_map/ppermute | solution.py:854
  79.6 14.6 %shard_map.268 = (bf16[256,1152]{1,0:T(8,128)(2,1)}, bf16[256,1152]{1,0:T(8,128)(2,1)}, bf16[256,384]{1,0:T(8,128)(2,1)}, bf16[256,384]{1,0:T(8,128)(2,1)}, bf16...) custom-call(s32[1,256]{1,0:T(1,128)} %copy-done.21, ...), custom_call_target="tpu_custom_call" | custom-call | flops 3321888768 | bytes 37565440 | tf_op jit(solution)/shard_map/pallas_call | solution.py:805
  94.9 1.9 collective-permute-done.9.refs_10_
  97.7 8.9 %shard_map.269 = (bf16[8,352,384]{2,1,0:T(8,128)(2,1)}, bf16[8,352,384]{2,1,0:T(8,128)(2,1)}) custom-call(s32[1,256]{1,0:T(1,128)} %copy-done.21, f32[8,768]{1,0:T(8,128)} %get-tuple-element.115.refs_1_, f32[8,3072]{1,0:T(8,128)} %get-tuple-element.116.refs_2_, bf16[256,2304]{1,0:T(8,128)(2,1)} %get-tuple-element.93.packed_hbm.refs_3_, ...), custom_call_target="tpu_custom_call" | custom-call | flops 2113929216 | bytes 11527168 | tf_op jit(solution)/shard_map/pallas_call | solution.py:805
  108.1 2.1 collective-permute-done.10.refs_2_
  112.1 5.7 %shard_map.270 = (bf16[8,240,384]{2,1,0:T(8,128)(2,1)}, bf16[8,240,384]{2,1,0:T(8,128)(2,1)}) custom-call(s32[1,256]{1,0:T(1,128)} %copy-done.21, bf16[256,1536]{1,0:T(8,128)(2,1)} %get-tuple-element.124.refs_1_, bf16[256,1536]{1,0:T(8,128)(2,1)} %copy-done.31, bf16[256,1920]{1,0:T(8,128)(2,1)} %get-tuple-element.125.refs_3_, bf16[256,1920]{1,0:T(8,128)(2,1)} %copy-done.27), custom_call_target="tpu_custom_call" | custom-call | flops 1509949440 | bytes 6489088 | tf_op jit(solution)/shard_map/pallas_call | solution.py:805
  122.0 10.5 %shard_map.271 = (bf16[256,768]{1,0:T(8,128)(2,1)}, f32[256,1536]{1,0:T(8,128)}, bf16[256,1536]{1,0:T(8,128)(2,1)}, f32[8,768]{1,0:T(8,128)}) custom-call(bf16[256,768]{1,0:T(8,128)(2,1)} %get-tuple-element.129.low_hbm, bf16[256,768]{1,0:T(8,128)(2,1)} %get-tuple-element.89.query_hbm, bf16[256,2688]{1,0:T(8,128)(2,1)} %get-tuple-element.90.packed_hbm.refs_3_, ...), custom_call_target="tpu_custom_call" | custom-call | flops 1308622848 | bytes 11821056 | tf_op jit(solution)/shard_map/pallas_call | solution.py:805
  133.7 2.8 %add_convert_fusion.1 = bf16[4,352,384]{2,1,0:T(8,128)(2,1)} fusion(bf16[8,352,384]{2,1,0:T(8,128)(2,1)} %collective-permute-done.13.refs_6_, bf16[8,352,384]{2,1,0:T(8,128)(2,1)} %get-tuple-element.122.refs_5_), kind=kLoop, calls=%fused_computation.1 | loop fusion | flops 2162688 | bytes 3244032 | tf_op jit(solution)/shard_map/convert_element_type | solution.py:860
  137.4 7.2 %shard_map.272 = (bf16[256,1152]{1,0:T(8,128)(2,1)}, bf16[256,1152]{1,0:T(8,128)(2,1)}, f32[256,768]{1,0:T(8,128)}, f32[8,768]{1,0:T(8,128)}) custom-call(s32[1,256]{1,0:T(1,128)} %copy-done.21, f32[2,768]{1,0:T(2,128)} %gain.9, f32[8,768]{1,0:T(8,128)} %get-tuple-element.134.dq_sum, f32[8,768]{1,0:T(8,128)} %get-tuple-element.135.vectors_two, ...), custom_call_target="tpu_custom_call" | custom-call | flops 905969664 | bytes 13057024 | tf_op jit(solution)/shard_map/pallas_call | solution.py:805
  146.4 3.1 %collective-permute-done.22.refs_1_ = bf16[8,240,384]{2,1,0:T(8,128)(2,1)} collective-permute-done((bf16[8,240,384]{2,1,0:T(8,128)(2,1)}, bf16[8,240,384]{2,1,0:T(8,128)(2,1)}, u32[]{:S(2)}, u32[]{:S(2)}) %collective-permute-start.22) | collective-permute-done | bytes 1474592 | tf_op jit(solution)/shard_map/ppermute | solution.py:854
  149.5 2.4 add_convert_fusion.2
  153.4 2.2 add_convert_fusion.3
  155.6 5.9 %shard_map.274 = (bf16[8,160,384]{2,1,0:T(8,128)(2,1)}, bf16[8,160,384]{2,1,0:T(8,128)(2,1)}) custom-call(s32[1,256]{1,0:T(1,128)} %copy-done.21, f32[8,768]{1,0:T(8,128)} %get-tuple-element.144.refs_1_, f32[8,3072]{1,0:T(8,128)} %get-tuple-element.145.refs_2_, bf16[256,2688]{1,0:T(8,128)(2,1)} %get-tuple-element.90.packed_hbm.refs_3_, ...), custom_call_target="tpu_custom_call" | custom-call | flops 905969664 | bytes 6022144 | tf_op jit(solution)/shard_map/pallas_call | solution.py:805
  162.2 12.5 %collective-permute-done.18.refs_7_ = bf16[4,352,384]{2,1,0:T(8,128)(2,1)} collective-permute-done((bf16[4,352,384]{2,1,0:T(8,128)(2,1)}, bf16[4,352,384]{2,1,0:T(8,128)(2,1)}, u32[]{:S(2)}, u32[]{:S(2)}) %collective-permute-start.18) | collective-permute-done | bytes 1081376 | tf_op jit(solution)/shard_map/ppermute | solution.py:854
  183.0 2.7 %collective-permute-done.19.refs_8_ = bf16[2,352,384]{2,1,0:T(8,128)(2,1)S(1)} collective-permute-done((bf16[2,352,384]{2,1,0:T(8,128)(2,1)S(1)}, bf16[2,352,384]{2,1,0:T(8,128)(2,1)S(1)}, u32[]{:S(2)}, u32[]{:S(2)}) %collective-permute-start.19) | collective-permute-done | bytes 540704 | tf_op jit(solution)/shard_map/ppermute | solution.py:854
  187.2 2.7 %collective-permute-start.20 = (bf16[1,352,384]{2,1,0:T(8,128)(2,1)S(1)}, bf16[1,352,384]{2,1,0:T(8,128)(2,1)S(1)}, u32[]{:S(2)}, u32[]{:S(2)}) collective-permute-start(bf16[1,352,384]{2,1,0:T(8,128)(2,1)S(1)} %add_convert_fusion.8), channel_id=1, source_target_pairs={{0,16},{1,17},{2,18},{3,19},{4,20},{5,21},{6,22},{7,23},{8,24},{9,... | collective-permute-start | bytes 811016 | tf_op jit(solution)/shard_map/ppermute | solution.py:854
  189.9 3.0 %collective-permute-done.16.refs_3_ = bf16[2,432,384]{2,1,0:T(8,128)(2,1)S(1)} collective-permute-done((bf16[2,432,384]{2,1,0:T(8,128)(2,1)S(1)}, bf16[2,432,384]{2,1,0:T(8,128)(2,1)S(1)}, u32[]{:S(2)}, u32[]{:S(2)}) %collective-permute-start.16) | collective-permute-done | bytes 663584 | tf_op jit(solution)/shard_map/ppermute | solution.py:854
  194.2 2.7 %collective-permute-start.17 = (bf16[1,432,384]{2,1,0:T(8,128)(2,1)S(1)}, bf16[1,432,384]{2,1,0:T(8,128)(2,1)S(1)}, u32[]{:S(2)}, u32[]{:S(2)}) collective-permute-start(bf16[1,432,384]{2,1,0:T(8,128)(2,1)S(1)} %add_convert_fusion.7), channel_id=1, source_target_pairs={{0,16},{1,17},{2,18},{3,19},{4,20},{5,21},{6,22},{7,23},{8,24},{9,... | collective-permute-start | bytes 995336 | tf_op jit(solution)/shard_map/ppermute | solution.py:854
  201.2 2.6 %collective-permute-start.25 = (bf16[1,240,384]{2,1,0:T(8,128)(2,1)S(1)}, bf16[1,240,384]{2,1,0:T(8,128)(2,1)S(1)}, u32[]{:S(2)}, u32[]{:S(2)}) collective-permute-start(bf16[1,240,384]{2,1,0:T(8,128)(2,1)S(1)} %add_convert_fusion.10), channel_id=1, source_target_pairs={{0,16},{1,17},{2,18},{3,19},{4,20},{5,21},{6,22},{7,23},{8,24},{9,... | collective-permute-start | bytes 552968 | tf_op jit(solution)/shard_map/ppermute | solution.py:854
  203.8 9.8 %collective-permute-done.20.refs_9_ = bf16[1,352,384]{2,1,0:T(8,128)(2,1)S(1)} collective-permute-done((bf16[1,352,384]{2,1,0:T(8,128)(2,1)S(1)}, bf16[1,352,384]{2,1,0:T(8,128)(2,1)S(1)}, u32[]{:S(2)}, u32[]{:S(2)}) %collective-permute-start.20) | collective-permute-done | bytes 270368 | tf_op jit(solution)/shard_map/ppermute | solution.py:854
  214.3 6.4 %collective-permute-done.17.refs_4_ = bf16[1,432,384]{2,1,0:T(8,128)(2,1)S(1)} collective-permute-done((bf16[1,432,384]{2,1,0:T(8,128)(2,1)S(1)}, bf16[1,432,384]{2,1,0:T(8,128)(2,1)S(1)}, u32[]{:S(2)}, u32[]{:S(2)}) %collective-permute-start.17) | collective-permute-done | bytes 331808 | tf_op jit(solution)/shard_map/ppermute | solution.py:854
  221.4 3.4 %shard_map.273 = (f32[400,384]{1,0:T(8,128)}, f32[400,384]{1,0:T(8,128)}) custom-call(bf16[8,432,384]{2,1,0:T(8,128)(2,1)} %get-tuple-element.104.refs_0_, bf16[8,432,384]{2,1,0:T(8,128)(2,1)} %copy-done.2, bf16[4,432,384]{2,1,0:T(8,128)(2,1)} %collective-permute-done.15.refs_2_, bf16[2,432,384]{2,1,0:T(8,128)(2,1)} %copy-done.8, ...), custom_call_target="tpu_custom_call" | custom-call | bytes 15077376 | tf_op jit(solution)/shard_map/pallas_call | solution.py:805
  226.2 8.2 %collective-permute-done.30.refs_9_ = bf16[1,160,384]{2,1,0:T(8,128)(2,1)S(1)} collective-permute-done((bf16[1,160,384]{2,1,0:T(8,128)(2,1)S(1)}, bf16[1,160,384]{2,1,0:T(8,128)(2,1)S(1)}, u32[]{:S(2)}, u32[]{:S(2)}) %collective-permute-start.30) | collective-permute-done | bytes 122912 | tf_op jit(solution)/shard_map/ppermute | solution.py:854
  235.1 2.6 %shard_map.275 = (f32[208,384]{1,0:T(8,128)}, f32[208,384]{1,0:T(8,128)}) custom-call(bf16[8,240,384]{2,1,0:T(8,128)(2,1)} %get-tuple-element.127.refs_0_, bf16[8,240,384]{2,1,0:T(8,128)(2,1)} %collective-permute-done.22.refs_1_, bf16[4,240,384]{2,1,0:T(8,128)(2,1)} %copy-done.6, bf16[2,240,384]{2,1,0:T(8,128)(2,1)} %copy-done.10, ...), custom_call_target="tpu_custom_call" | custom-call | bytes 7704576 | tf_op jit(solution)/shard_map/pallas_call | solution.py:805
  240.2 2.7 %shard_map.276 = (f32[2,24,2304]{2,1,0:T(8,128)}, f32[2,24,768]{2,1,0:T(8,128)}, f32[2,24,3072]{2,1,0:T(8,128)}, f32[2,96,768]{2,1,0:T(8,128)}, f32[2,24]{1,0:T(...) custom-call(f32[400,384]{1,0:T(8,128)} %get-tuple-element.140.refs_0, ...), custom_call_target="tpu_custom_call" | custom-call | bytes 3639552 | tf_op jit(solution)/shard_map/pallas_call | solution.py:805
  (127 shorter events, 44.3 us)
Async XLA Ops:
  5.4 3.5 %collective-permute-start.1 = (bf16[256,2688]{1,0:T(8,128)(2,1)}, bf16[256,2688]{1,0:T(8,128)(2,1)S(1)}, u32[]{:S(2)}, u32[]{:S(2)}) collective-permute-start(bf16[256,2688]{1,0:T(8,128)(2,1)} %get-tuple-element.90.packed_hbm.refs_3_), channel_id=1, source_target_pairs={{0,1},{1,0},{2,3},{3,2},{4,5},{5,4},{6,7},{7,6},{8,9},{9,8},{10,11... | collective-permute-start | bytes 4128776 | tf_op jit(solution)/shard_map/ppermute | solution.py:817
  6.0 2.6 %collective-permute-start = (s32[1,256]{1,0:T(1,128)S(1)}, s32[1,256]{1,0:T(1,128)S(1)}, u32[]{:S(2)}, u32[]{:S(2)}) collective-permute-start(s32[1,256]{1,0:T(1,128)S(1)} %multiply_add_fusion.code.refs_0_.gate), channel_id=1, source_target_pairs={{0,1},{1,0},{2,3},{3,2},{4,5},{5,4},{6,7},{7,6},{8,9},{9,8},{10,11... | collective-permute-start | bytes 3080 | tf_op jit(solution)/shard_map/ppermute | solution.py:817
  27.7 3.1 %collective-permute-start.2 = (bf16[256,2304]{1,0:T(8,128)(2,1)}, bf16[256,2304]{1,0:T(8,128)(2,1)S(1)}, u32[]{:S(2)}, u32[]{:S(2)}) collective-permute-start(bf16[256,2304]{1,0:T(8,128)(2,1)} %get-tuple-element.93.packed_hbm.refs_3_), channel_id=1, source_target_pairs={{0,1},{1,0},{2,3},{3,2},{4,5},{5,4},{6,7},{7,6},{8,9},{9,8},{10,11... | collective-permute-start | bytes 3538952 | tf_op jit(solution)/shard_map/ppermute | solution.py:817
  52.7 12.3 %collective-permute-start.3 = (bf16[256,3072]{1,0:T(8,128)(2,1)}, bf16[256,3072]{1,0:T(8,128)(2,1)S(1)}, u32[]{:S(2)}, u32[]{:S(2)}) collective-permute-start(bf16[256,3072]{1,0:T(8,128)(2,1)} %get-tuple-element.99.refs_1_), channel_id=1, source_target_pairs={{0,1},{1,0},{2,3},{3,2},{4,5},{5,4},{6,7},{7,6},{8,9},{9,8},{10,11... | collective-permute-start | bytes 4718600 | tf_op jit(solution)/shard_map/ppermute | solution.py:817
  53.2 11.9 %collective-permute-start.5 = (bf16[256,1920]{1,0:T(8,128)(2,1)}, bf16[256,1920]{1,0:T(8,128)(2,1)S(1)}, u32[]{:S(2)}, u32[]{:S(2)}) collective-permute-start(bf16[256,1920]{1,0:T(8,128)(2,1)} %get-tuple-element.103), channel_id=1, source_target_pairs={{0,1},{1,0},{2,3},{3,2},{4,5},{5,4},{6,7},{7,6},{8,9},{9,8},{10,11... | collective-permute-start | bytes 2949128 | tf_op jit(solution)/shard_map/ppermute | solution.py:817
  53.3 11.7 %collective-permute-start.4 = (bf16[256,1536]{1,0:T(8,128)(2,1)}, bf16[256,1536]{1,0:T(8,128)(2,1)S(1)}, u32[]{:S(2)}, u32[]{:S(2)}) collective-permute-start(bf16[256,1536]{1,0:T(8,128)(2,1)} %get-tuple-element.101.refs_5_), channel_id=1, source_target_pairs={{0,1},{1,0},{2,3},{3,2},{4,5},{5,4},{6,7},{7,6},{8,9},{9,8},{10,11... | collective-permute-start | bytes 2359304 | tf_op jit(solution)/shard_map/ppermute | solution.py:817
  64.4 14.3 %collective-permute-start.6 = (bf16[256,1536]{1,0:T(8,128)(2,1)}, bf16[256,1536]{1,0:T(8,128)(2,1)S(1)}, u32[]{:S(2)}, u32[]{:S(2)}) collective-permute-start(bf16[256,1536]{1,0:T(8,128)(2,1)} %get-tuple-element.109), channel_id=1, source_target_pairs={{0,1},{1,0},{2,3},{3,2},{4,5},{5,4},{6,7},{7,6},{8,9},{9,8},{10,11... | collective-permute-start | bytes 2359304 | tf_op jit(solution)/shard_map/ppermute | solution.py:817
  64.6 30.3 %collective-permute-start.8 = (bf16[256,3072]{1,0:T(8,128)(2,1)S(1)}, bf16[256,3072]{1,0:T(8,128)(2,1)}, u32[]{:S(2)}, u32[]{:S(2)}) collective-permute-start(bf16[256,3072]{1,0:T(8,128)(2,1)S(1)} %copy-done.25), channel_id=1, source_target_pairs={{0,1},{1,0},{2,3},{3,2},{4,5},{5,4},{6,7},{7,6},{8,9},{9,8},{10,11... | collective-permute-start | bytes 4718600 | tf_op jit(solution)/shard_map/ppermute | solution.py:817
  76.0 42.6 %collective-permute-start.12 = (bf16[8,432,384]{2,1,0:T(8,128)(2,1)}, bf16[8,432,384]{2,1,0:T(8,128)(2,1)S(1)}, u32[]{:S(2)}, u32[]{:S(2)}) collective-permute-start(bf16[8,432,384]{2,1,0:T(8,128)(2,1)} %get-tuple-element.128), channel_id=1, source_target_pairs={{0,2},{1,5},{2,0},{3,7},{4,6},{5,1},{6,4},{7,3},{8,10},{9,13},{10,... | collective-permute-start | bytes 7962632 | tf_op jit(solution)/shard_map/ppermute | solution.py:854
  94.2 2.6 %collective-permute-start.7 = (bf16[256,1152]{1,0:T(8,128)(2,1)}, bf16[256,1152]{1,0:T(8,128)(2,1)S(1)}, u32[]{:S(2)}, u32[]{:S(2)}) collective-permute-start(bf16[256,1152]{1,0:T(8,128)(2,1)} %get-tuple-element.118), channel_id=1, source_target_pairs={{0,1},{1,0},{2,3},{3,2},{4,5},{5,4},{6,7},{7,6},{8,9},{9,8},{10,11... | collective-permute-start | bytes 1769480 | tf_op jit(solution)/shard_map/ppermute | solution.py:817
  94.4 2.4 collective-permute-start.9
  94.8 15.4 %collective-permute-start.11 = (bf16[256,1920]{1,0:T(8,128)(2,1)}, bf16[256,1920]{1,0:T(8,128)(2,1)S(1)}, u32[]{:S(2)}, u32[]{:S(2)}) collective-permute-start(bf16[256,1920]{1,0:T(8,128)(2,1)} %get-tuple-element.126), channel_id=1, source_target_pairs={{0,1},{1,0},{2,3},{3,2},{4,5},{5,4},{6,7},{7,6},{8,9},{9,8},{10,11... | collective-permute-start | bytes 2949128 | tf_op jit(solution)/shard_map/ppermute | solution.py:817
  106.6 27.1 %collective-permute-start.13 = (bf16[8,352,384]{2,1,0:T(8,128)(2,1)}, bf16[8,352,384]{2,1,0:T(8,128)(2,1)}, u32[]{:S(2)}, u32[]{:S(2)}) collective-permute-start(bf16[8,352,384]{2,1,0:T(8,128)(2,1)} %get-tuple-element.132), channel_id=1, source_target_pairs={{0,2},{1,5},{2,0},{3,7},{4,6},{5,1},{6,4},{7,3},{8,10},{9,13},{10,... | collective-permute-start | bytes 6488072 | tf_op jit(solution)/shard_map/ppermute | solution.py:854
  107.9 2.3 collective-permute-start.10
  117.7 31.7 %collective-permute-start.22 = (bf16[8,240,384]{2,1,0:T(8,128)(2,1)}, bf16[8,240,384]{2,1,0:T(8,128)(2,1)}, u32[]{:S(2)}, u32[]{:S(2)}) collective-permute-start(bf16[8,240,384]{2,1,0:T(8,128)(2,1)} %get-tuple-element.142), channel_id=1, source_target_pairs={{0,2},{1,5},{2,0},{3,7},{4,6},{5,1},{6,4},{7,3},{8,10},{9,13},{10,... | collective-permute-start | bytes 4423688 | tf_op jit(solution)/shard_map/ppermute | solution.py:854
  120.3 33.1 %collective-permute-start.15 = (bf16[4,432,384]{2,1,0:T(8,128)(2,1)}, bf16[4,432,384]{2,1,0:T(8,128)(2,1)}, u32[]{:S(2)}, u32[]{:S(2)}) collective-permute-start(bf16[4,432,384]{2,1,0:T(8,128)(2,1)} %add_convert_fusion), channel_id=1, source_target_pairs={{0,8},{1,9},{2,10},{3,11},{4,12},{5,13},{6,14},{7,15},{8,0},{9,1},... | collective-permute-start | bytes 3981320 | tf_op jit(solution)/shard_map/ppermute | solution.py:854
  132.5 4.0 %collective-permute-start.14 = (bf16[256,1536]{1,0:T(8,128)(2,1)}, bf16[256,1536]{1,0:T(8,128)(2,1)S(1)}, u32[]{:S(2)}, u32[]{:S(2)}) collective-permute-start(bf16[256,1536]{1,0:T(8,128)(2,1)} %get-tuple-element.137), channel_id=1, source_target_pairs={{0,1},{1,0},{2,3},{3,2},{4,5},{5,4},{6,7},{7,6},{8,9},{9,8},{10,11... | collective-permute-start | bytes 2359304 | tf_op jit(solution)/shard_map/ppermute | solution.py:817
  144.6 11.0 %collective-permute-start.26 = (bf16[256,1152]{1,0:T(8,128)(2,1)}, bf16[256,1152]{1,0:T(8,128)(2,1)}, u32[]{:S(2)}, u32[]{:S(2)}) collective-permute-start(bf16[256,1152]{1,0:T(8,128)(2,1)} %get-tuple-element.147), channel_id=1, source_target_pairs={{0,1},{1,0},{2,3},{3,2},{4,5},{5,4},{6,7},{7,6},{8,9},{9,8},{10,11... | collective-permute-start | bytes 1769480 | tf_op jit(solution)/shard_map/ppermute | solution.py:817
  144.7 30.0 %collective-permute-start.18 = (bf16[4,352,384]{2,1,0:T(8,128)(2,1)}, bf16[4,352,384]{2,1,0:T(8,128)(2,1)}, u32[]{:S(2)}, u32[]{:S(2)}) collective-permute-start(bf16[4,352,384]{2,1,0:T(8,128)(2,1)} %add_convert_fusion.1), channel_id=1, source_target_pairs={{0,8},{1,9},{2,10},{3,11},{4,12},{5,13},{6,14},{7,15},{8,0},{9,1},... | collective-permute-start | bytes 3244040 | tf_op jit(solution)/shard_map/ppermute | solution.py:854
  151.9 26.5 %collective-permute-start.23 = (bf16[4,240,384]{2,1,0:T(8,128)(2,1)}, bf16[4,240,384]{2,1,0:T(8,128)(2,1)S(1)}, u32[]{:S(2)}, u32[]{:S(2)}) collective-permute-start(bf16[4,240,384]{2,1,0:T(8,128)(2,1)} %add_convert_fusion.2), channel_id=1, source_target_pairs={{0,4},{1,3},{2,6},{3,1},{4,0},{5,7},{6,2},{7,5},{8,12},{9,11},{10,... | collective-permute-start | bytes 2211848 | tf_op jit(solution)/shard_map/ppermute | solution.py:854
  161.6 20.0 %collective-permute-start.27 = (bf16[8,160,384]{2,1,0:T(8,128)(2,1)}, bf16[8,160,384]{2,1,0:T(8,128)(2,1)S(1)}, u32[]{:S(2)}, u32[]{:S(2)}) collective-permute-start(bf16[8,160,384]{2,1,0:T(8,128)(2,1)} %get-tuple-element.149), channel_id=1, source_target_pairs={{0,2},{1,5},{2,0},{3,7},{4,6},{5,1},{6,4},{7,3},{8,10},{9,13},{10,... | collective-permute-start | bytes 2949128 | tf_op jit(solution)/shard_map/ppermute | solution.py:854
  176.3 9.4 %collective-permute-start.19 = (bf16[2,352,384]{2,1,0:T(8,128)(2,1)S(1)}, bf16[2,352,384]{2,1,0:T(8,128)(2,1)S(1)}, u32[]{:S(2)}, u32[]{:S(2)}) collective-permute-start(bf16[2,352,384]{2,1,0:T(8,128)(2,1)S(1)} %add_convert_fusion.4), channel_id=1, source_target_pairs={{0,4},{1,3},{2,6},{3,1},{4,0},{5,7},{6,2},{7,5},{8,12},{9,11},{10,... | collective-permute-start | bytes 1622024 | tf_op jit(solution)/shard_map/ppermute | solution.py:854
  177.6 15.2 %collective-permute-start.16 = (bf16[2,432,384]{2,1,0:T(8,128)(2,1)S(1)}, bf16[2,432,384]{2,1,0:T(8,128)(2,1)S(1)}, u32[]{:S(2)}, u32[]{:S(2)}) collective-permute-start(bf16[2,432,384]{2,1,0:T(8,128)(2,1)S(1)} %copy-done.13), channel_id=1, source_target_pairs={{0,4},{1,3},{2,6},{3,1},{4,0},{5,7},{6,2},{7,5},{8,12},{9,11},{10,... | collective-permute-start | bytes 1990664 | tf_op jit(solution)/shard_map/ppermute | solution.py:854
  179.9 20.0 %collective-permute-start.24 = (bf16[2,240,384]{2,1,0:T(8,128)(2,1)S(1)}, bf16[2,240,384]{2,1,0:T(8,128)(2,1)S(1)}, u32[]{:S(2)}, u32[]{:S(2)}) collective-permute-start(bf16[2,240,384]{2,1,0:T(8,128)(2,1)S(1)} %add_convert_fusion.6), channel_id=1, source_target_pairs={{0,8},{1,9},{2,10},{3,11},{4,12},{5,13},{6,14},{7,15},{8,0},{9,1},... | collective-permute-start | bytes 1105928 | tf_op jit(solution)/shard_map/ppermute | solution.py:854
  181.7 16.4 %collective-permute-start.28 = (bf16[4,160,384]{2,1,0:T(8,128)(2,1)S(1)}, bf16[4,160,384]{2,1,0:T(8,128)(2,1)S(1)}, u32[]{:S(2)}, u32[]{:S(2)}) collective-permute-start(bf16[4,160,384]{2,1,0:T(8,128)(2,1)S(1)} %add_convert_fusion.5), channel_id=1, source_target_pairs={{0,4},{1,3},{2,6},{3,1},{4,0},{5,7},{6,2},{7,5},{8,12},{9,11},{10,... | collective-permute-start | bytes 1474568 | tf_op jit(solution)/shard_map/ppermute | solution.py:854
  187.2 26.4 %collective-permute-start.20 = (bf16[1,352,384]{2,1,0:T(8,128)(2,1)S(1)}, bf16[1,352,384]{2,1,0:T(8,128)(2,1)S(1)}, u32[]{:S(2)}, u32[]{:S(2)}) collective-permute-start(bf16[1,352,384]{2,1,0:T(8,128)(2,1)S(1)} %add_convert_fusion.8), channel_id=1, source_target_pairs={{0,16},{1,17},{2,18},{3,19},{4,20},{5,21},{6,22},{7,23},{8,24},{9,... | collective-permute-start | bytes 811016 | tf_op jit(solution)/shard_map/ppermute | solution.py:854
  194.2 26.5 %collective-permute-start.17 = (bf16[1,432,384]{2,1,0:T(8,128)(2,1)S(1)}, bf16[1,432,384]{2,1,0:T(8,128)(2,1)S(1)}, u32[]{:S(2)}, u32[]{:S(2)}) collective-permute-start(bf16[1,432,384]{2,1,0:T(8,128)(2,1)S(1)} %add_convert_fusion.7), channel_id=1, source_target_pairs={{0,16},{1,17},{2,18},{3,19},{4,20},{5,21},{6,22},{7,23},{8,24},{9,... | collective-permute-start | bytes 995336 | tf_op jit(solution)/shard_map/ppermute | solution.py:854
  198.2 26.7 %collective-permute-start.29 = (bf16[2,160,384]{2,1,0:T(8,128)(2,1)S(1)}, bf16[2,160,384]{2,1,0:T(8,128)(2,1)S(1)}, u32[]{:S(2)}, u32[]{:S(2)}) collective-permute-start(bf16[2,160,384]{2,1,0:T(8,128)(2,1)S(1)} %add_convert_fusion.9), channel_id=1, source_target_pairs={{0,8},{1,9},{2,10},{3,11},{4,12},{5,13},{6,14},{7,15},{8,0},{9,1},... | collective-permute-start | bytes 737288 | tf_op jit(solution)/shard_map/ppermute | solution.py:854
  201.2 25.0 %collective-permute-start.25 = (bf16[1,240,384]{2,1,0:T(8,128)(2,1)S(1)}, bf16[1,240,384]{2,1,0:T(8,128)(2,1)S(1)}, u32[]{:S(2)}, u32[]{:S(2)}) collective-permute-start(bf16[1,240,384]{2,1,0:T(8,128)(2,1)S(1)} %add_convert_fusion.10), channel_id=1, source_target_pairs={{0,16},{1,17},{2,18},{3,19},{4,20},{5,21},{6,22},{7,23},{8,24},{9,... | collective-permute-start | bytes 552968 | tf_op jit(solution)/shard_map/ppermute | solution.py:854
  224.8 12.9 %collective-permute-start.21 = (f32[400,384]{1,0:T(8,128)}, f32[400,384]{1,0:T(8,128)S(1)}, u32[]{:S(2)}, u32[]{:S(2)}) collective-permute-start(f32[400,384]{1,0:T(8,128)} %get-tuple-element.141), channel_id=1, source_target_pairs={{0,1},{1,0},{2,3},{3,2},{4,5},{5,4},{6,7},{7,6},{8,9},{9,8},{10,11... | collective-permute-start | bytes 1843208 | tf_op jit(solution)/shard_map/ppermute | solution.py:817
  226.1 8.3 %collective-permute-start.30 = (bf16[1,160,384]{2,1,0:T(8,128)(2,1)S(1)}, bf16[1,160,384]{2,1,0:T(8,128)(2,1)S(1)}, u32[]{:S(2)}, u32[]{:S(2)}) collective-permute-start(bf16[1,160,384]{2,1,0:T(8,128)(2,1)S(1)} %add_convert_fusion.11), channel_id=1, source_target_pairs={{0,16},{1,17},{2,18},{3,19},{4,20},{5,21},{6,22},{7,23},{8,24},{9,... | collective-permute-start | bytes 368648 | tf_op jit(solution)/shard_map/ppermute | solution.py:854
  237.6 1.9 collective-permute-start.31
  (34 other events, 247.3 us)
where the time goes:
time: 244 us; the launch traced here: 243 us
  Pallas kernels  125 us (51%)
  waiting for transfers between devices  59.3 us (24%)
  starting transfers between devices  29 us (12%)
  other arithmetic  17.6 us (7%)
  local copies, waits for them, and re-layouts  11.3 us (5%)
    pallas_call x14, Pallas kernels, call(): pl.pallas_call(kernel, out_shape=tuple(outs), in_specs=list(ins), out_spe...  125 us
    ppermute x16, waiting for transfers between devices, move(): self.parts.append(lax.ppermute(sent, ('row', 'tok'), pairs))  48 us
    ppermute x16, starting transfers between devices, move(): self.parts.append(lax.ppermute(sent, ('row', 'tok'), pairs))  25.2 us
    convert_element_type x12, other arithmetic, next(): sent = sent.astype(self.parts[0].dtype)  17.6 us
    unnamed x68, local copies, waits for them, and re-layouts  11.3 us
    ppermute x16, waiting for transfers between devices, swap_cores(): return lax.ppermute(array, 'tok', [(0, 1), (1, 0)])  11.3 us
  transfers between devices with their start and end apart: 32, of which 15 were waited for; matrix products, arithmetic and copies ran while one was open for 7% of the time, Pallas kernels for 32%

commit v1 on v0

--- a/solution.py
+++ b/solution.py
@@ -13,10 +13,10 @@
 masked_score = -1e30
 head_size = 64
 lanes = 128
-plan = {"F2": (), "jd": (), "u0": (), "B1b": (0,), "B2": (1,), "j0": (0, 2), "tail": (), "first": 1, "orders": "zzzrr", "done": 2}
-forward_unroll = 1
+plan = {"F2": (), "jd": (0,), "u0": (1,), "B1b": (0,), "B2": (0, 1), "j0": (2, 3, 1), "tail": (), "first": 0, "orders": "zzzrr", "done": 3}
+forward_unroll = 3
 backward_unroll = 1
-mlp_unroll = 1
+mlp_unroll = 2
 f32 = jnp.float32
 bf16 = jnp.bfloat16
 VMEM = pl.BlockSpec(memory_space=pltpu.VMEM)
@@ -620,103 +620,124 @@
     kept_hbm, sent_hbm = refs[count : count + 2]
     refs = refs[count + 2 :]
     lefts, rights = refs[: len(plan)], refs[len(plan) : 2 * len(plan)]
-    block, slot_sems, sems = refs[2 * len(plan) :]
-    copies = Copies(sems)
+    turned, block, slot_sems, left_sems, sems = refs[2 * len(plan) :]
     columns = block.shape[2]
     half = chips // 2
     steps = chips.bit_length() - 1
-    waits = []
-    for item, left, right in zip(plan, lefts, rights):
-        own, far, at, at_far, size, right_own, right_far, right_at, right_at_far, strips, row = item
-        piece = min(size, 768)
-        wait = []
-        for first in range(0, size, piece):
-            for side, array, start in ((0, own, at), (1, far, at_far)):
-                wait.append(
-                    copies.bring(
-                        arrays[array].at[:, pl.ds(start + first, piece)],
-                        left.at[side, :, pl.ds(first, piece)],
-                    )
-                )
-        for side, array, start in ((0, right_own, right_at), (1, right_far, right_at_far)):
-            window = pl.ds(start, strips * columns)
-            wait.append(copies.bring(arrays[array].at[:, window], right.at[side]))
-        waits.append(wait)
-    slots = []
-    for chip in range(chips):
+    bits = [
+        jnp.where(core == 0, step_bit(order, step, 0), step_bit(order, step, 1))
+        for step in range(steps)
+    ]
+
+    def slot_of(chip):
         apart = chip ^ me
         slot = 0
-        for step in range(steps):
-            bit = jnp.where(core == 0, step_bit(order, step, 0), step_bit(order, step, 1))
+        for bit in bits:
             slot = slot * 2 + ((apart >> bit) & 1)
-        slots.append(slot)
-    outgoing = []
-
-    def send_rows(chip, row, count):
-        sem = slot_sems.at[len(outgoing)]
+        return slot
+
+    def left_copy(number, index, side):
+        own, far, at, at_far, size = plan[number][:5]
+        first = pl.multiple_of(index * 768, 768)
+        return pltpu.make_async_copy(
+            arrays[(own, far)[side]].at[:, pl.ds((at, at_far)[side] + first, 768)],
+            lefts[number].at[side, :, pl.ds(first, 768)],
+            left_sems.at[number, side, index],
+        )
+
+    def right_copy(number, side):
+        own, far, at, at_far, strips = plan[number][5:10]
+        window = pl.ds((at, at_far)[side], strips * columns)
+        return pltpu.make_async_copy(
+            arrays[(own, far)[side]].at[:, window], rights[number].at[side], sems.at[number, side]
+        )
+
+    for number, item in enumerate(plan):
+        for index in range(item[4] // 768):
+            for side in range(2):
+                left_copy(number, index, side).start()
+            if not index:
+                for side in range(2):
+                    right_copy(number, side).start()
+
+    def row_copy(number, chip, row, count):
+        slot = slot_of(chip)
         window = pl.ds(row, count)
-        source = block.at[slots[chip], window]
-
-        @pl.when(slots[chip] >= half)
+        sem = slot_sems.at[number, chip]
+
+        @pl.when(slot >= half)
         def _():
-            target = sent_hbm.at[slots[chip] - half, window]
-            pltpu.make_async_copy(source, target, sem).start()
-
-        @pl.when(slots[chip] < half)
+            target = sent_hbm.at[slot - half, window]
+            pltpu.make_async_copy(block.at[slot, window], target, sem).start()
+
+        @pl.when(slot < half)
         def _():
-            pltpu.make_async_copy(source, kept_hbm.at[slots[chip], window], sem).start()
-
-        outgoing.append(pltpu.make_async_copy(source, kept_hbm.at[0, window], sem))
-
+            pltpu.make_async_copy(block.at[slot, window], kept_hbm.at[slot, window], sem).start()
+
+    depth = 16
     if vector_row:
-        depth = 16
         width, inner = vectors.shape[1], up_sum.shape[1]
 
-        def one_slot(slot, carry):
-            apart = sum(
-                ((slot >> (steps - 1 - step)) & 1)
-                << jnp.where(core == 0, step_bit(order, step, 0), step_bit(order, step, 1))
-                for step in range(steps)
-            )
-            chip = me ^ apart
+        def one_chip(chip, carry):
             short = pltpu.roll(vectors[...], width - chip * (width // chips), axis=1)
             wide = pltpu.roll(up_sum[...], inner - chip * (inner // chips), axis=1)
-            block[slot, vector_row : vector_row + depth, :] = jnp.concatenate(
+            block[slot_of(chip), vector_row : vector_row + depth, :] = jnp.concatenate(
                 [short[:, :columns], wide[:, :columns]], axis=0
             ).astype(bf16)
             return carry
 
-        lax.fori_loop(0, chips, one_slot, 0)
-    for item, left, right, wait in zip(plan, lefts, rights, waits):
+        lax.fori_loop(0, chips, one_chip, 0)
+    counts = []
+    for number, item in enumerate(plan):
         size, strips, row = item[4], item[9], item[10]
+        left, right = lefts[number], rights[number]
+        rows = left.shape[1]
         part = size // chips
-        piece = min(size, 768)
-        for first in range(0, size, piece):
-            flipped = []
+        some = 768 // part
+        count = strips * part + (depth if vector_row == row + strips * part else 0)
+        counts.append((row, count))
+
+        def one_piece(index, carry, number=number, left=left, right=right, strips=strips, row=row):
             for side in range(2):
-                wait[first // piece * 2 + side].wait()
-                flipped.append(left[side, :, first : first + piece].T)
-            if not first:
-                wait[-2].wait()
-                wait[-1].wait()
-            for strip in range(strips):
-                window = slice(strip * columns, (strip + 1) * columns)
-                product = dot(flipped[0], right[0, :, window]) + dot(
-                    flipped[1], right[1, :, window]
-                )
-                product = product.astype(bf16)
-                for cut in range(0, piece, part):
-                    slot = slots[(first + cut) // part]
-                    block[slot, row + strip * part : row + (strip + 1) * part, :] = product[
-                        cut : cut + part
-                    ]
-            for cut in range(0, piece, part):
-                with_them = vector_row == row + strips * part
-                send_rows(
-                    (first + cut) // part, row, strips * part + (depth if with_them else 0)
-                )
-    for copy in outgoing:
-        copy.wait()
+                left_copy(number, index, side).wait()
+                first = pl.multiple_of(index * 768, 768)
+                turned[:, side * rows : (side + 1) * rows] = left[side, :, pl.ds(first, 768)].T
+
+            @pl.when(index == 0)
+            def _():
+                for side in range(2):
+                    right_copy(number, side).wait()
+
+            def one_strip(strip, carry):
+                window = pl.ds(pl.multiple_of(strip * columns, columns), columns)
+                product = dot(turned[:, :rows], right[0, :, window])
+                product += dot(turned[:, rows:], right[1, :, window])
+                at = pl.multiple_of(row + strip * part, 16)
+                for one in range(some):
+                    block[slot_of(index * some + one), pl.ds(at, part), :] = product[
+                        one * part : (one + 1) * part
+                    ].astype(bf16)
+                return carry
+
+            lax.fori_loop(0, strips, one_strip, 0)
+
+            def one_send(one, carry):
+                row_copy(number, index * some + one, row, count)
+                return carry
+
+            lax.fori_loop(0, some, one_send, 0)
+            return carry
+
+        lax.fori_loop(0, size // 768, one_piece, 0)
+    for number, (row, count) in enumerate(counts):
+
+        def one_wait(chip, carry, number=number, window=pl.ds(row, count)):
+            pltpu.make_async_copy(
+                block.at[0, window], kept_hbm.at[0, window], slot_sems.at[number, chip]
+            ).wait()
+            return carry
+
+        lax.fori_loop(0, chips, one_wait, 0)
 
 
 def sum_kernel(groups, *refs):
@@ -796,7 +817,7 @@
                 outputs[11][layer : layer + 1] = wide[0:1, :wide_size]
 
 
-def call(kernel, outs, ins, scratch, *arrays, flops=0, out_specs=None, limit=58):
+def call(kernel, outs, ins, scratch, *arrays, flops=0, out_specs=None, limit=63):
     out_specs = tuple(out_specs or (ANY for _ in outs))
     count = sum(math.prod(a.shape) * a.dtype.itemsize for a in list(arrays) + list(outs))
     held = [kept for kept in scratch if kept.memory_space == pltpu.VMEM]
@@ -1215,9 +1236,11 @@
             [vm(2, rows, item[4]) for item in plan]
             + [vm(2, rows, item[9] * columns) for item in plan]
             + [
+                vm(768, 2 * rows),
                 vm(chips, row, columns),
-                dma((chips * len(plan),)),
-                dma((sum(2 * max(1, item[4] // 768) + 2 for item in plan),)),
+                dma((len(plan), chips)),
+                dma((len(plan), 2, max(item[4] for item in plan) // 768)),
+                dma((len(plan), 2)),
             ],
             after(code, *gate_arrays),
             *vectors[:2],

time: 244 us -> 237 us (0.971)
  other arithmetic: 17.6 us -> 26.3 us
  waiting for transfers between devices: 59.3 us -> 51.8 us
  local copies, waits for them, and re-layouts: 11.3 us -> 4.03 us
    convert_element_type x12 -> x15, other arithmetic: 17.6 us -> 26.3 us  [next(): sent = sent.astype(self.parts[0].dtype)]
    unnamed x68 -> x40, local copies, waits for them, and re-layouts: 11.3 us -> 4.03 us
    ppermute x16 -> x20, waiting for transfers between devices: 48 us -> 44 us  [move(): self.parts.append(lax.ppermute(sent, ('row', 'tok'), pairs))]
    ppermute x16, waiting for transfers between devices: 11.3 us -> 7.72 us  [swap_cores(): return lax.ppermute(array, 'tok', [(0, 1), (1, 0)])]
    pallas_call x14 -> x15, Pallas kernels: 125 us -> 123 us  [call(): pl.pallas_call(kernel, out_shape=tuple(outs), in_specs=list(ins), out_spe...]
    ppermute x16 -> x20, starting transfers between devices: 25.2 us -> 25.6 us  [move(): self.parts.append(lax.ppermute(sent, ('row', 'tok'), pairs))]
  transfers between devices with their start and end apart: 32 -> 36, of which waited for: 15 -> 11; matrix products, arithmetic and copies ran while one was open for 7% -> 11% of each run, Pallas kernels for 32% -> 35%
where the time goes in v1:
time: 237 us; the launch traced here: 236 us
  Pallas kernels  123 us (52%)
  waiting for transfers between devices  51.8 us (22%)
  starting transfers between devices  29.6 us (12%)
  other arithmetic  26.3 us (11%)
  local copies, waits for them, and re-layouts  4.03 us (2%)
    pallas_call x15, Pallas kernels, call(): pl.pallas_call(kernel, out_shape=tuple(outs), in_specs=list(ins), out_spe...  123 us
    ppermute x20, waiting for transfers between devices, move(): self.parts.append(lax.ppermute(sent, ('row', 'tok'), pairs))  44 us
    convert_element_type x15, other arithmetic, next(): sent = sent.astype(self.parts[0].dtype)  26.3 us
    ppermute x20, starting transfers between devices, move(): self.parts.append(lax.ppermute(sent, ('row', 'tok'), pairs))  25.6 us
    ppermute x16, waiting for transfers between devices, swap_cores(): return lax.ppermute(array, 'tok', [(0, 1), (1, 0)])  7.72 us
  transfers between devices with their start and end apart: 36, of which 11 were waited for; matrix products, arithmetic and copies ran while one was open for 11% of the time, Pallas kernels for 35%

profile of v1, /device:TPU:0, one launch (start us, length us, event | category | flops | bytes accessed | tf_op | source)
XLA Modules:
  0.0 236.2 jit_solution(5895944847476365165)
XLA Ops:
  0.7 4.8 %shard_map.263 = (bf16[256,768]{1,0:T(8,128)(2,1)}, bf16[256,2688]{1,0:T(8,128)(2,1)}, bf16[256,384]{1,0:T(8,128)(2,1)}) custom-call(f32[2,768]{1,0:T(2,128)} %gain.9, f32[2,768]{1,0:T(2,128)} %next_shift.1, f32[2,2,768]{2,1,0:T(2,128)} %joint_bias.1, bf16[256,768]{1,0:T(8,128)(2,1)} %bitcast.4, bf16[2,768,2304]{2,1,0:T(8,128)(2,1)} %joint_hbm.5, ...), custom_call_target="tpu_custom_call" | custom-call | flops 905969664 | bytes 9854976 | tf_op jit(solution)/shard_map/pallas_call | solution.py:826
  6.1 2.5 %collective-permute-done.code_far = s32[1,256]{1,0:T(1,128)S(1)} collective-permute-done((s32[1,256]{1,0:T(1,128)S(1)}, s32[1,256]{1,0:T(1,128)S(1)}, u32[]{:S(2)}, u32[]{:S(2)}) %collective-permute-start) | collective-permute-done | bytes 1056 | tf_op jit(solution)/shard_map/ppermute | solution.py:838
  9.2 14.6 %shard_map.264 = (bf16[256,1536]{1,0:T(8,128)(2,1)}, bf16[256,3072]{1,0:T(8,128)(2,1)}, bf16[12,256,512]{2,1,0:T(8,128)(2,1)}, f32[256,768]{1,0:T(8,128)}, bf16[...) custom-call(s32[1,256]{1,0:T(1,128)} %copy-done.14, ...), custom_call_target="tpu_custom_call" | custom-call | flops 4026531840 | bytes 42149888 | tf_op jit(solution)/shard_map/pallas_call | solution.py:826
  24.1 2.9 %collective-permute-done.2.far_hbm.refs_4_ = bf16[256,2304]{1,0:T(8,128)(2,1)} collective-permute-done((bf16[256,2304]{1,0:T(8,128)(2,1)}, bf16[256,2304]{1,0:T(8,128)(2,1)}, u32[]{:S(2)}, u32[]{:S(2)}) %collective-permute-start.2) | collective-permute-done | bytes 1179680 | tf_op jit(solution)/shard_map/ppermute | solution.py:838
  27.1 17.8 %shard_map.265 = (bf16[256,1536]{1,0:T(8,128)(2,1)}, bf16[256,3072]{1,0:T(8,128)(2,1)}, bf16[12,256,512]{2,1,0:T(8,128)(2,1)}, bf16[256,768]{1,0:T(8,128)(2,1)},...) custom-call(s32[1,256]{1,0:T(1,128)} %copy-done.14, ...), custom_call_target="tpu_custom_call" | custom-call | flops 5536481280 | bytes 34383872 | tf_op jit(solution)/shard_map/pallas_call | solution.py:826
  45.8 10.5 %shard_map.266 = (bf16[256,768]{1,0:T(8,128)(2,1)}, f32[256,1536]{1,0:T(8,128)}, bf16[256,1536]{1,0:T(8,128)(2,1)}, f32[8,768]{1,0:T(8,128)}) custom-call(bf16[256,768]{1,0:T(8,128)(2,1)} %get-tuple-element.98.low_hbm, bf16[256,768]{1,0:T(8,128)(2,1)} %get-tuple-element.95.query_hbm, bf16[256,2304]{1,0:T(8,128)(2,1)} %get-tuple-element.96.packed_hbm.refs_3_, ...), custom_call_target="tpu_custom_call" | custom-call | flops 1308622848 | bytes 11427840 | tf_op jit(solution)/shard_map/pallas_call | solution.py:826
  56.9 6.3 %shard_map.267 = (bf16[8,192,384]{2,1,0:T(8,128)(2,1)}, bf16[8,192,384]{2,1,0:T(8,128)(2,1)}) custom-call(s32[1,256]{1,0:T(1,128)} %copy-done.14, bf16[256,3072]{1,0:T(8,128)(2,1)} %get-tuple-element.102.refs_1_, bf16[256,3072]{1,0:T(8,128)(2,1)} %collective-permute-done.3.refs_2_, bf16[256,384]{1,0:T(8,128)(2,1)} %get-tuple-element.103.refs_3_, ...), custom_call_target="tpu_custom_call" | custom-call | flops 1207959552 | bytes 7078912 | tf_op jit(solution)/shard_map/pallas_call | solution.py:826
  63.2 2.7 %collective-permute-start.7 = (bf16[8,192,384]{2,1,0:T(8,128)(2,1)}, bf16[8,192,384]{2,1,0:T(8,128)(2,1)}, u32[]{:S(2)}, u32[]{:S(2)}) collective-permute-start(bf16[8,192,384]{2,1,0:T(8,128)(2,1)} %get-tuple-element.119), channel_id=1, source_target_pairs={{0,2},{1,5},{2,0},{3,7},{4,6},{5,1},{6,4},{7,3},{8,10},{9,13},{10,... | collective-permute-start | bytes 3538952 | tf_op jit(solution)/shard_map/ppermute | solution.py:875
  65.9 6.3 %shard_map.268 = (bf16[8,240,384]{2,1,0:T(8,128)(2,1)}, bf16[8,240,384]{2,1,0:T(8,128)(2,1)}) custom-call(s32[1,256]{1,0:T(1,128)} %copy-done.14, bf16[256,1536]{1,0:T(8,128)(2,1)} %get-tuple-element.106.refs_1_, bf16[256,1536]{1,0:T(8,128)(2,1)} %collective-permute-done.4.refs_2_, bf16[256,1920]{1,0:T(8,128)(2,1)} %get-tuple-element.107.refs_3_, ...), custom_call_target="tpu_custom_call" | custom-call | flops 1509949440 | bytes 6489088 | tf_op jit(solution)/shard_map/pallas_call | solution.py:826
  73.2 14.3 %shard_map.269 = (bf16[256,1152]{1,0:T(8,128)(2,1)}, bf16[256,1152]{1,0:T(8,128)(2,1)}, bf16[256,384]{1,0:T(8,128)(2,1)}, bf16[256,384]{1,0:T(8,128)(2,1)}, bf16...) custom-call(s32[1,256]{1,0:T(1,128)} %copy-done.14, ...), custom_call_target="tpu_custom_call" | custom-call | flops 3321888768 | bytes 37565440 | tf_op jit(solution)/shard_map/pallas_call | solution.py:826
  88.2 2.2 add_convert_fusion.3
  91.8 10.0 %shard_map.270 = (bf16[8,352,384]{2,1,0:T(8,128)(2,1)}, bf16[8,352,384]{2,1,0:T(8,128)(2,1)}) custom-call(s32[1,256]{1,0:T(1,128)} %copy-done.14, f32[8,768]{1,0:T(8,128)} %get-tuple-element.121.refs_1_, f32[8,3072]{1,0:T(8,128)} %get-tuple-element.122.refs_2_, bf16[256,2304]{1,0:T(8,128)(2,1)} %get-tuple-element.96.packed_hbm.refs_3_, ...), custom_call_target="tpu_custom_call" | custom-call | flops 2113929216 | bytes 11527168 | tf_op jit(solution)/shard_map/pallas_call | solution.py:826
  101.7 2.0 collective-permute-start.21
  105.3 2.5 %add_convert_fusion.2 = bf16[4,240,384]{2,1,0:T(8,128)(2,1)} fusion(bf16[8,240,384]{2,1,0:T(8,128)(2,1)} %collective-permute-done.11.refs_6_, bf16[8,240,384]{2,1,0:T(8,128)(2,1)} %get-tuple-element.109.refs_5_), kind=kLoop, calls=%fused_computation.2 | loop fusion | flops 1474560 | bytes 2211840 | tf_op jit(solution)/shard_map/convert_element_type | solution.py:881
  108.3 6.3 %shard_map.271 = (bf16[8,240,384]{2,1,0:T(8,128)(2,1)}, bf16[8,240,384]{2,1,0:T(8,128)(2,1)}) custom-call(s32[1,256]{1,0:T(1,128)} %copy-done.14, bf16[256,1536]{1,0:T(8,128)(2,1)} %get-tuple-element.131.refs_1_, bf16[256,1536]{1,0:T(8,128)(2,1)} %collective-permute-done.12.refs_2_, bf16[256,1920]{1,0:T(8,128)(2,1)} %get-tuple-element.132.refs_3_, ...), custom_call_target="tpu_custom_call" | custom-call | flops 1509949440 | bytes 6489088 | tf_op jit(solution)/shard_map/pallas_call | solution.py:826
  114.8 5.5 %collective-permute-done.14.refs_2_ = bf16[4,192,384]{2,1,0:T(8,128)(2,1)} collective-permute-done((bf16[4,192,384]{2,1,0:T(8,128)(2,1)}, bf16[4,192,384]{2,1,0:T(8,128)(2,1)}, u32[]{:S(2)}, u32[]{:S(2)}) %collective-permute-start.14) | collective-permute-done | bytes 589856 | tf_op jit(solution)/shard_map/ppermute | solution.py:875
  120.3 2.0 add_convert_fusion.8
  123.8 10.5 %shard_map.272 = (bf16[256,768]{1,0:T(8,128)(2,1)}, f32[256,1536]{1,0:T(8,128)}, bf16[256,1536]{1,0:T(8,128)(2,1)}, f32[8,768]{1,0:T(8,128)}) custom-call(bf16[256,768]{1,0:T(8,128)(2,1)} %get-tuple-element.135.low_hbm, bf16[256,768]{1,0:T(8,128)(2,1)} %get-tuple-element.92.query_hbm, bf16[256,2688]{1,0:T(8,128)(2,1)} %get-tuple-element.93.packed_hbm.refs_3_, ...), custom_call_target="tpu_custom_call" | custom-call | flops 1308622848 | bytes 11821056 | tf_op jit(solution)/shard_map/pallas_call | solution.py:826
  136.3 2.2 add_convert_fusion.7
  139.0 7.2 %shard_map.273 = (bf16[256,1152]{1,0:T(8,128)(2,1)}, bf16[256,1152]{1,0:T(8,128)(2,1)}, f32[256,768]{1,0:T(8,128)}, f32[8,768]{1,0:T(8,128)}) custom-call(s32[1,256]{1,0:T(1,128)} %copy-done.14, f32[2,768]{1,0:T(2,128)} %gain.9, f32[8,768]{1,0:T(8,128)} %get-tuple-element.139.dq_sum, f32[8,768]{1,0:T(8,128)} %get-tuple-element.140.vectors_two, ...), custom_call_target="tpu_custom_call" | custom-call | flops 905969664 | bytes 13057024 | tf_op jit(solution)/shard_map/pallas_call | solution.py:826
  146.5 2.9 %add_convert_fusion = bf16[4,352,384]{2,1,0:T(8,128)(2,1)} fusion(bf16[8,352,384]{2,1,0:T(8,128)(2,1)} %collective-permute-done.21.refs_11_, bf16[8,352,384]{2,1,0:T(8,128)(2,1)} %get-tuple-element.128.refs_10_), kind=kLoop, calls=%fused_computation | loop fusion | flops 2162688 | bytes 3244032 | tf_op jit(solution)/shard_map/convert_element_type | solution.py:881
  152.9 2.3 add_convert_fusion.1
  155.2 6.0 %shard_map.275 = (bf16[8,160,384]{2,1,0:T(8,128)(2,1)}, bf16[8,160,384]{2,1,0:T(8,128)(2,1)}) custom-call(s32[1,256]{1,0:T(1,128)} %copy-done.14, f32[8,768]{1,0:T(8,128)} %get-tuple-element.150.refs_1_, f32[8,3072]{1,0:T(8,128)} %get-tuple-element.151.refs_2_, bf16[256,2688]{1,0:T(8,128)(2,1)} %get-tuple-element.93.packed_hbm.refs_3_, ...), custom_call_target="tpu_custom_call" | custom-call | flops 905969664 | bytes 6022144 | tf_op jit(solution)/shard_map/pallas_call | solution.py:826
  163.6 12.2 %collective-permute-done.22.refs_12_ = bf16[4,352,384]{2,1,0:T(8,128)(2,1)} collective-permute-done((bf16[4,352,384]{2,1,0:T(8,128)(2,1)}, bf16[4,352,384]{2,1,0:T(8,128)(2,1)}, u32[]{:S(2)}, u32[]{:S(2)}) %collective-permute-start.22) | collective-permute-done | bytes 1081376 | tf_op jit(solution)/shard_map/ppermute | solution.py:875
  178.9 2.6 %collective-permute-start.18 = (bf16[1,192,384]{2,1,0:T(8,128)(2,1)S(1)}, bf16[1,192,384]{2,1,0:T(8,128)(2,1)S(1)}, u32[]{:S(2)}, u32[]{:S(2)}) collective-permute-start(bf16[1,192,384]{2,1,0:T(8,128)(2,1)S(1)} %copy-done.11), channel_id=1, source_target_pairs={{0,16},{1,17},{2,18},{3,19},{4,20},{5,21},{6,22},{7,23},{8,24},{9,... | collective-permute-start | bytes 442376 | tf_op jit(solution)/shard_map/ppermute | solution.py:875
  181.8 4.1 %collective-permute-done.31.refs_6_ = bf16[8,160,384]{2,1,0:T(8,128)(2,1)S(1)} collective-permute-done((bf16[8,160,384]{2,1,0:T(8,128)(2,1)}, bf16[8,160,384]{2,1,0:T(8,128)(2,1)S(1)}, u32[]{:S(2)}, u32[]{:S(2)}) %collective-permute-start.31) | collective-permute-done | bytes 983072 | tf_op jit(solution)/shard_map/ppermute | solution.py:875
  190.5 2.7 %collective-permute-start.24 = (bf16[1,352,384]{2,1,0:T(8,128)(2,1)S(1)}, bf16[1,352,384]{2,1,0:T(8,128)(2,1)}, u32[]{:S(2)}, u32[]{:S(2)}) collective-permute-start(bf16[1,352,384]{2,1,0:T(8,128)(2,1)S(1)} %add_convert_fusion.9), channel_id=1, source_target_pairs={{0,16},{1,17},{2,18},{3,19},{4,20},{5,21},{6,22},{7,23},{8,24},{9,... | collective-permute-start | bytes 811016 | tf_op jit(solution)/shard_map/ppermute | solution.py:875
  196.8 12.4 %collective-permute-done.28.refs_3_ = bf16[2,240,384]{2,1,0:T(8,128)(2,1)S(1)} collective-permute-done((bf16[2,240,384]{2,1,0:T(8,128)(2,1)S(1)}, bf16[2,240,384]{2,1,0:T(8,128)(2,1)S(1)}, u32[]{:S(2)}, u32[]{:S(2)}) %collective-permute-start.28) | collective-permute-done | bytes 368672 | tf_op jit(solution)/shard_map/ppermute | solution.py:875
  213.5 3.4 %shard_map.274 = (f32[400,384]{1,0:T(8,128)}, f32[400,384]{1,0:T(8,128)}) custom-call(bf16[8,192,384]{2,1,0:T(8,128)(2,1)} %get-tuple-element.104.refs_0_, bf16[8,192,384]{2,1,0:T(8,128)(2,1)} %collective-permute-done.7.refs_1_, bf16[4,192,384]{2,1,0:T(8,128)(2,1)} %collective-permute-done.14.refs_2_, bf16[2,192,384]{2,1,0:T(8,128)(2,1)} %collective-permute-done.15.refs_3_, ...), custom_call_target="tpu_custom_call" | custom-call | bytes 15077376 | tf_op jit(solution)/shard_map/pallas_call | solution.py:826
  219.9 7.5 %collective-permute-done.34.refs_9_ = bf16[1,160,384]{2,1,0:T(8,128)(2,1)S(1)} collective-permute-done((bf16[1,160,384]{2,1,0:T(8,128)(2,1)S(1)}, bf16[1,160,384]{2,1,0:T(8,128)(2,1)S(1)}, u32[]{:S(2)}, u32[]{:S(2)}) %collective-permute-start.34) | collective-permute-done | bytes 122912 | tf_op jit(solution)/shard_map/ppermute | solution.py:875
  228.1 2.6 %shard_map.276 = (f32[208,384]{1,0:T(8,128)}, f32[208,384]{1,0:T(8,128)}) custom-call(bf16[8,240,384]{2,1,0:T(8,128)(2,1)} %get-tuple-element.134.refs_0_, bf16[8,240,384]{2,1,0:T(8,128)(2,1)} %collective-permute-done.26.refs_1_, bf16[4,240,384]{2,1,0:T(8,128)(2,1)} %copy-done.3, bf16[2,240,384]{2,1,0:T(8,128)(2,1)} %copy-done.7, ...), custom_call_target="tpu_custom_call" | custom-call | bytes 7704576 | tf_op jit(solution)/shard_map/pallas_call | solution.py:826
  233.3 2.7 %shard_map.277 = (f32[2,24,2304]{2,1,0:T(8,128)}, f32[2,24,768]{2,1,0:T(8,128)}, f32[2,24,3072]{2,1,0:T(8,128)}, f32[2,96,768]{2,1,0:T(8,128)}, f32[2,24]{1,0:T(...) custom-call(f32[400,384]{1,0:T(8,128)} %get-tuple-element.146.refs_0, ...), custom_call_target="tpu_custom_call" | custom-call | bytes 3639552 | tf_op jit(solution)/shard_map/pallas_call | solution.py:826
  (111 shorter events, 40.4 us)
Async XLA Ops:
  5.4 3.6 %collective-permute-start.1 = (bf16[256,2688]{1,0:T(8,128)(2,1)}, bf16[256,2688]{1,0:T(8,128)(2,1)}, u32[]{:S(2)}, u32[]{:S(2)}) collective-permute-start(bf16[256,2688]{1,0:T(8,128)(2,1)} %get-tuple-element.93.packed_hbm.refs_3_), channel_id=1, source_target_pairs={{0,1},{1,0},{2,3},{3,2},{4,5},{5,4},{6,7},{7,6},{8,9},{9,8},{10,11... | collective-permute-start | bytes 4128776 | tf_op jit(solution)/shard_map/ppermute | solution.py:838
  44.9 12.0 %collective-permute-start.3 = (bf16[256,3072]{1,0:T(8,128)(2,1)}, bf16[256,3072]{1,0:T(8,128)(2,1)}, u32[]{:S(2)}, u32[]{:S(2)}) collective-permute-start(bf16[256,3072]{1,0:T(8,128)(2,1)} %get-tuple-element.102.refs_1_), channel_id=1, source_target_pairs={{0,1},{1,0},{2,3},{3,2},{4,5},{5,4},{6,7},{7,6},{8,9},{9,8},{10,11... | collective-permute-start | bytes 4718600 | tf_op jit(solution)/shard_map/ppermute | solution.py:838
  45.2 20.7 %collective-permute-start.5 = (bf16[256,1920]{1,0:T(8,128)(2,1)}, bf16[256,1920]{1,0:T(8,128)(2,1)}, u32[]{:S(2)}, u32[]{:S(2)}) collective-permute-start(bf16[256,1920]{1,0:T(8,128)(2,1)} %get-tuple-element.108), channel_id=1, source_target_pairs={{0,1},{1,0},{2,3},{3,2},{4,5},{5,4},{6,7},{7,6},{8,9},{9,8},{10,11... | collective-permute-start | bytes 2949128 | tf_op jit(solution)/shard_map/ppermute | solution.py:838
  45.5 20.4 %collective-permute-start.4 = (bf16[256,1536]{1,0:T(8,128)(2,1)}, bf16[256,1536]{1,0:T(8,128)(2,1)}, u32[]{:S(2)}, u32[]{:S(2)}) collective-permute-start(bf16[256,1536]{1,0:T(8,128)(2,1)} %get-tuple-element.106.refs_1_), channel_id=1, source_target_pairs={{0,1},{1,0},{2,3},{3,2},{4,5},{5,4},{6,7},{7,6},{8,9},{9,8},{10,11... | collective-permute-start | bytes 2359304 | tf_op jit(solution)/shard_map/ppermute | solution.py:838
  56.3 16.0 %collective-permute-start.6 = (bf16[256,1536]{1,0:T(8,128)(2,1)}, bf16[256,1536]{1,0:T(8,128)(2,1)S(1)}, u32[]{:S(2)}, u32[]{:S(2)}) collective-permute-start(bf16[256,1536]{1,0:T(8,128)(2,1)} %get-tuple-element.114), channel_id=1, source_target_pairs={{0,1},{1,0},{2,3},{3,2},{4,5},{5,4},{6,7},{7,6},{8,9},{9,8},{10,11... | collective-permute-start | bytes 2359304 | tf_op jit(solution)/shard_map/ppermute | solution.py:838
  56.6 33.9 %collective-permute-start.9 = (bf16[256,3072]{1,0:T(8,128)(2,1)}, bf16[256,3072]{1,0:T(8,128)(2,1)}, u32[]{:S(2)}, u32[]{:S(2)}) collective-permute-start(bf16[256,3072]{1,0:T(8,128)(2,1)} %get-tuple-element.125.refs_7_), channel_id=1, source_target_pairs={{0,1},{1,0},{2,3},{3,2},{4,5},{5,4},{6,7},{7,6},{8,9},{9,8},{10,11... | collective-permute-start | bytes 4718600 | tf_op jit(solution)/shard_map/ppermute | solution.py:838
  63.2 25.0 %collective-permute-start.7 = (bf16[8,192,384]{2,1,0:T(8,128)(2,1)}, bf16[8,192,384]{2,1,0:T(8,128)(2,1)}, u32[]{:S(2)}, u32[]{:S(2)}) collective-permute-start(bf16[8,192,384]{2,1,0:T(8,128)(2,1)} %get-tuple-element.119), channel_id=1, source_target_pairs={{0,2},{1,5},{2,0},{3,7},{4,6},{5,1},{6,4},{7,3},{8,10},{9,13},{10,... | collective-permute-start | bytes 3538952 | tf_op jit(solution)/shard_map/ppermute | solution.py:875
  72.2 33.1 %collective-permute-start.11 = (bf16[8,240,384]{2,1,0:T(8,128)(2,1)}, bf16[8,240,384]{2,1,0:T(8,128)(2,1)}, u32[]{:S(2)}, u32[]{:S(2)}) collective-permute-start(bf16[8,240,384]{2,1,0:T(8,128)(2,1)} %get-tuple-element.129), channel_id=1, source_target_pairs={{0,2},{1,5},{2,0},{3,7},{4,6},{5,1},{6,4},{7,3},{8,10},{9,13},{10,... | collective-permute-start | bytes 4423688 | tf_op jit(solution)/shard_map/ppermute | solution.py:875
  87.6 3.3 %collective-permute-start.8 = (bf16[256,1152]{1,0:T(8,128)(2,1)}, bf16[256,1152]{1,0:T(8,128)(2,1)S(1)}, u32[]{:S(2)}, u32[]{:S(2)}) collective-permute-start(bf16[256,1152]{1,0:T(8,128)(2,1)} %get-tuple-element.124), channel_id=1, source_target_pairs={{0,1},{1,0},{2,3},{3,2},{4,5},{5,4},{6,7},{7,6},{8,9},{9,8},{10,11... | collective-permute-start | bytes 1769480 | tf_op jit(solution)/shard_map/ppermute | solution.py:838
  88.1 20.1 %collective-permute-start.13 = (bf16[256,1920]{1,0:T(8,128)(2,1)}, bf16[256,1920]{1,0:T(8,128)(2,1)}, u32[]{:S(2)}, u32[]{:S(2)}) collective-permute-start(bf16[256,1920]{1,0:T(8,128)(2,1)} %get-tuple-element.133), channel_id=1, source_target_pairs={{0,1},{1,0},{2,3},{3,2},{4,5},{5,4},{6,7},{7,6},{8,9},{9,8},{10,11... | collective-permute-start | bytes 2949128 | tf_op jit(solution)/shard_map/ppermute | solution.py:838
  90.4 17.8 %collective-permute-start.12 = (bf16[256,1536]{1,0:T(8,128)(2,1)}, bf16[256,1536]{1,0:T(8,128)(2,1)}, u32[]{:S(2)}, u32[]{:S(2)}) collective-permute-start(bf16[256,1536]{1,0:T(8,128)(2,1)} %get-tuple-element.131.refs_1_), channel_id=1, source_target_pairs={{0,1},{1,0},{2,3},{3,2},{4,5},{5,4},{6,7},{7,6},{8,9},{9,8},{10,11... | collective-permute-start | bytes 2359304 | tf_op jit(solution)/shard_map/ppermute | solution.py:838
  101.7 44.8 %collective-permute-start.21 = (bf16[8,352,384]{2,1,0:T(8,128)(2,1)}, bf16[8,352,384]{2,1,0:T(8,128)(2,1)}, u32[]{:S(2)}, u32[]{:S(2)}) collective-permute-start(bf16[8,352,384]{2,1,0:T(8,128)(2,1)} %get-tuple-element.145), channel_id=1, source_target_pairs={{0,2},{1,5},{2,0},{3,7},{4,6},{5,1},{6,4},{7,3},{8,10},{9,13},{10,... | collective-permute-start | bytes 6488072 | tf_op jit(solution)/shard_map/ppermute | solution.py:875
  103.8 16.5 %collective-permute-start.14 = (bf16[4,192,384]{2,1,0:T(8,128)(2,1)}, bf16[4,192,384]{2,1,0:T(8,128)(2,1)}, u32[]{:S(2)}, u32[]{:S(2)}) collective-permute-start(bf16[4,192,384]{2,1,0:T(8,128)(2,1)} %add_convert_fusion.3), channel_id=1, source_target_pairs={{0,8},{1,9},{2,10},{3,11},{4,12},{5,13},{6,14},{7,15},{8,0},{9,1},... | collective-permute-start | bytes 1769480 | tf_op jit(solution)/shard_map/ppermute | solution.py:875
  107.8 28.5 %collective-permute-start.16 = (bf16[4,240,384]{2,1,0:T(8,128)(2,1)}, bf16[4,240,384]{2,1,0:T(8,128)(2,1)S(1)}, u32[]{:S(2)}, u32[]{:S(2)}) collective-permute-start(bf16[4,240,384]{2,1,0:T(8,128)(2,1)} %add_convert_fusion.2), channel_id=1, source_target_pairs={{0,8},{1,9},{2,10},{3,11},{4,12},{5,13},{6,14},{7,15},{8,0},{9,1},... | collective-permute-start | bytes 2211848 | tf_op jit(solution)/shard_map/ppermute | solution.py:875
  114.6 38.3 %collective-permute-start.26 = (bf16[8,240,384]{2,1,0:T(8,128)(2,1)}, bf16[8,240,384]{2,1,0:T(8,128)(2,1)}, u32[]{:S(2)}, u32[]{:S(2)}) collective-permute-start(bf16[8,240,384]{2,1,0:T(8,128)(2,1)} %get-tuple-element.148), channel_id=1, source_target_pairs={{0,2},{1,5},{2,0},{3,7},{4,6},{5,1},{6,4},{7,3},{8,10},{9,13},{10,... | collective-permute-start | bytes 4423688 | tf_op jit(solution)/shard_map/ppermute | solution.py:875
  122.3 12.1 %collective-permute-start.15 = (bf16[2,192,384]{2,1,0:T(8,128)(2,1)}, bf16[2,192,384]{2,1,0:T(8,128)(2,1)}, u32[]{:S(2)}, u32[]{:S(2)}) collective-permute-start(bf16[2,192,384]{2,1,0:T(8,128)(2,1)} %add_convert_fusion.8), channel_id=1, source_target_pairs={{0,4},{1,3},{2,6},{3,1},{4,0},{5,7},{6,2},{7,5},{8,12},{9,11},{10,... | collective-permute-start | bytes 884744 | tf_op jit(solution)/shard_map/ppermute | solution.py:875
  134.3 4.7 %collective-permute-start.17 = (bf16[256,1536]{1,0:T(8,128)(2,1)}, bf16[256,1536]{1,0:T(8,128)(2,1)}, u32[]{:S(2)}, u32[]{:S(2)}) collective-permute-start(bf16[256,1536]{1,0:T(8,128)(2,1)} %get-tuple-element.142), channel_id=1, source_target_pairs={{0,1},{1,0},{2,3},{3,2},{4,5},{5,4},{6,7},{7,6},{8,9},{9,8},{10,11... | collective-permute-start | bytes 2359304 | tf_op jit(solution)/shard_map/ppermute | solution.py:838
  138.5 12.5 %collective-permute-start.19 = (bf16[2,240,384]{2,1,0:T(8,128)(2,1)}, bf16[2,240,384]{2,1,0:T(8,128)(2,1)}, u32[]{:S(2)}, u32[]{:S(2)}) collective-permute-start(bf16[2,240,384]{2,1,0:T(8,128)(2,1)} %add_convert_fusion.7), channel_id=1, source_target_pairs={{0,4},{1,3},{2,6},{3,1},{4,0},{5,7},{6,2},{7,5},{8,12},{9,11},{10,... | collective-permute-start | bytes 1105928 | tf_op jit(solution)/shard_map/ppermute | solution.py:875
  146.2 8.9 %collective-permute-start.30 = (bf16[256,1152]{1,0:T(8,128)(2,1)}, bf16[256,1152]{1,0:T(8,128)(2,1)}, u32[]{:S(2)}, u32[]{:S(2)}) collective-permute-start(bf16[256,1152]{1,0:T(8,128)(2,1)} %get-tuple-element.153), channel_id=1, source_target_pairs={{0,1},{1,0},{2,3},{3,2},{4,5},{5,4},{6,7},{7,6},{8,9},{9,8},{10,11... | collective-permute-start | bytes 1769480 | tf_op jit(solution)/shard_map/ppermute | solution.py:838
  149.5 26.3 %collective-permute-start.22 = (bf16[4,352,384]{2,1,0:T(8,128)(2,1)}, bf16[4,352,384]{2,1,0:T(8,128)(2,1)}, u32[]{:S(2)}, u32[]{:S(2)}) collective-permute-start(bf16[4,352,384]{2,1,0:T(8,128)(2,1)} %add_convert_fusion), channel_id=1, source_target_pairs={{0,8},{1,9},{2,10},{3,11},{4,12},{5,13},{6,14},{7,15},{8,0},{9,1},... | collective-permute-start | bytes 3244040 | tf_op jit(solution)/shard_map/ppermute | solution.py:875
  161.2 24.7 %collective-permute-start.31 = (bf16[8,160,384]{2,1,0:T(8,128)(2,1)}, bf16[8,160,384]{2,1,0:T(8,128)(2,1)S(1)}, u32[]{:S(2)}, u32[]{:S(2)}) collective-permute-start(bf16[8,160,384]{2,1,0:T(8,128)(2,1)} %get-tuple-element.155), channel_id=1, source_target_pairs={{0,2},{1,5},{2,0},{3,7},{4,6},{5,1},{6,4},{7,3},{8,10},{9,13},{10,... | collective-permute-start | bytes 2949128 | tf_op jit(solution)/shard_map/ppermute | solution.py:875
  162.6 24.8 %collective-permute-start.27 = (bf16[4,240,384]{2,1,0:T(8,128)(2,1)}, bf16[4,240,384]{2,1,0:T(8,128)(2,1)S(1)}, u32[]{:S(2)}, u32[]{:S(2)}) collective-permute-start(bf16[4,240,384]{2,1,0:T(8,128)(2,1)} %add_convert_fusion.1), channel_id=1, source_target_pairs={{0,4},{1,3},{2,6},{3,1},{4,0},{5,7},{6,2},{7,5},{8,12},{9,11},{10,... | collective-permute-start | bytes 2211848 | tf_op jit(solution)/shard_map/ppermute | solution.py:875
  177.4 11.6 %collective-permute-start.23 = (bf16[2,352,384]{2,1,0:T(8,128)(2,1)S(1)}, bf16[2,352,384]{2,1,0:T(8,128)(2,1)S(1)}, u32[]{:S(2)}, u32[]{:S(2)}) collective-permute-start(bf16[2,352,384]{2,1,0:T(8,128)(2,1)S(1)} %add_convert_fusion.4), channel_id=1, source_target_pairs={{0,4},{1,3},{2,6},{3,1},{4,0},{5,7},{6,2},{7,5},{8,12},{9,11},{10,... | collective-permute-start | bytes 1622024 | tf_op jit(solution)/shard_map/ppermute | solution.py:875
  178.9 33.9 %collective-permute-start.18 = (bf16[1,192,384]{2,1,0:T(8,128)(2,1)S(1)}, bf16[1,192,384]{2,1,0:T(8,128)(2,1)S(1)}, u32[]{:S(2)}, u32[]{:S(2)}) collective-permute-start(bf16[1,192,384]{2,1,0:T(8,128)(2,1)S(1)} %copy-done.11), channel_id=1, source_target_pairs={{0,16},{1,17},{2,18},{3,19},{4,20},{5,21},{6,22},{7,23},{8,24},{9,... | collective-permute-start | bytes 442376 | tf_op jit(solution)/shard_map/ppermute | solution.py:875
  181.5 31.3 %collective-permute-start.20 = (bf16[1,240,384]{2,1,0:T(8,128)(2,1)S(1)}, bf16[1,240,384]{2,1,0:T(8,128)(2,1)}, u32[]{:S(2)}, u32[]{:S(2)}) collective-permute-start(bf16[1,240,384]{2,1,0:T(8,128)(2,1)S(1)} %copy-done.10), channel_id=1, source_target_pairs={{0,16},{1,17},{2,18},{3,19},{4,20},{5,21},{6,22},{7,23},{8,24},{9,... | collective-permute-start | bytes 552968 | tf_op jit(solution)/shard_map/ppermute | solution.py:875
  186.1 8.9 %collective-permute-start.32 = (bf16[4,160,384]{2,1,0:T(8,128)(2,1)S(1)}, bf16[4,160,384]{2,1,0:T(8,128)(2,1)S(1)}, u32[]{:S(2)}, u32[]{:S(2)}) collective-permute-start(bf16[4,160,384]{2,1,0:T(8,128)(2,1)S(1)} %add_convert_fusion.5), channel_id=1, source_target_pairs={{0,4},{1,3},{2,6},{3,1},{4,0},{5,7},{6,2},{7,5},{8,12},{9,11},{10,... | collective-permute-start | bytes 1474568 | tf_op jit(solution)/shard_map/ppermute | solution.py:875
  188.9 20.4 %collective-permute-start.28 = (bf16[2,240,384]{2,1,0:T(8,128)(2,1)S(1)}, bf16[2,240,384]{2,1,0:T(8,128)(2,1)S(1)}, u32[]{:S(2)}, u32[]{:S(2)}) collective-permute-start(bf16[2,240,384]{2,1,0:T(8,128)(2,1)S(1)} %add_convert_fusion.6), channel_id=1, source_target_pairs={{0,8},{1,9},{2,10},{3,11},{4,12},{5,13},{6,14},{7,15},{8,0},{9,1},... | collective-permute-start | bytes 1105928 | tf_op jit(solution)/shard_map/ppermute | solution.py:875
  190.5 23.0 %collective-permute-start.24 = (bf16[1,352,384]{2,1,0:T(8,128)(2,1)S(1)}, bf16[1,352,384]{2,1,0:T(8,128)(2,1)}, u32[]{:S(2)}, u32[]{:S(2)}) collective-permute-start(bf16[1,352,384]{2,1,0:T(8,128)(2,1)S(1)} %add_convert_fusion.9), channel_id=1, source_target_pairs={{0,16},{1,17},{2,18},{3,19},{4,20},{5,21},{6,22},{7,23},{8,24},{9,... | collective-permute-start | bytes 811016 | tf_op jit(solution)/shard_map/ppermute | solution.py:875
  195.8 21.2 %collective-permute-start.33 = (bf16[2,160,384]{2,1,0:T(8,128)(2,1)}, bf16[2,160,384]{2,1,0:T(8,128)(2,1)}, u32[]{:S(2)}, u32[]{:S(2)}) collective-permute-start(bf16[2,160,384]{2,1,0:T(8,128)(2,1)} %add_convert_fusion.10), channel_id=1, source_target_pairs={{0,8},{1,9},{2,10},{3,11},{4,12},{5,13},{6,14},{7,15},{8,0},{9,1},... | collective-permute-start | bytes 737288 | tf_op jit(solution)/shard_map/ppermute | solution.py:875
  211.2 8.7 %collective-permute-start.29 = (bf16[1,240,384]{2,1,0:T(8,128)(2,1)}, bf16[1,240,384]{2,1,0:T(8,128)(2,1)}, u32[]{:S(2)}, u32[]{:S(2)}) collective-permute-start(bf16[1,240,384]{2,1,0:T(8,128)(2,1)} %add_convert_fusion.11), channel_id=1, source_target_pairs={{0,16},{1,17},{2,18},{3,19},{4,20},{5,21},{6,22},{7,23},{8,24},{9,... | collective-permute-start | bytes 552968 | tf_op jit(solution)/shard_map/ppermute | solution.py:875
  216.9 15.6 %collective-permute-start.25 = (f32[400,384]{1,0:T(8,128)}, f32[400,384]{1,0:T(8,128)}, u32[]{:S(2)}, u32[]{:S(2)}) collective-permute-start(f32[400,384]{1,0:T(8,128)} %get-tuple-element.147), channel_id=1, source_target_pairs={{0,1},{1,0},{2,3},{3,2},{4,5},{5,4},{6,7},{7,6},{8,9},{9,8},{10,11... | collective-permute-start | bytes 1843208 | tf_op jit(solution)/shard_map/ppermute | solution.py:838
  218.1 9.3 %collective-permute-start.34 = (bf16[1,160,384]{2,1,0:T(8,128)(2,1)S(1)}, bf16[1,160,384]{2,1,0:T(8,128)(2,1)S(1)}, u32[]{:S(2)}, u32[]{:S(2)}) collective-permute-start(bf16[1,160,384]{2,1,0:T(8,128)(2,1)S(1)} %add_convert_fusion.14), channel_id=1, source_target_pairs={{0,16},{1,17},{2,18},{3,19},{4,20},{5,21},{6,22},{7,23},{8,24},{9,... | collective-permute-start | bytes 368648 | tf_op jit(solution)/shard_map/ppermute | solution.py:875
  (24 other events, 186.9 us)

commit v2 on v1

--- a/solution.py
+++ b/solution.py
@@ -206,18 +206,18 @@
     width = tokens.shape[1]
     half = width // 2
     first = copies.bring(tokens_hbm, tokens)
+    thirds = copies.thirds(weight_hbm.at[0], weight, (1, 2, 0))
     third = copies.bring(grad_hbm, grad)
-    thirds = copies.thirds(weight_hbm.at[0], weight, (1, 2, 0))
     core = lax.axis_index("tok")
     first.wait()
+    emit_project(tokens[...].astype(f32), 0, gain, shift, bias, weight, thirds, normed, query, kv)
+    copies.send(kv, packed_hbm.at[:, pl.ds(0, 2 * width)])
     third.wait()
     copies.send(
         grad.at[:, pl.ds(pl.multiple_of((1 - core) * half, half), half)],
         packed_hbm.at[:, pl.ds(3 * width, half)],
     )
     copies.send(grad.at[:, pl.ds(pl.multiple_of(core * half, half), half)], kept_hbm)
-    emit_project(tokens[...].astype(f32), 0, gain, shift, bias, weight, thirds, normed, query, kv)
-    copies.send(kv, packed_hbm.at[:, pl.ds(0, 2 * width)])
     copies.send(normed, packed_hbm.at[:, pl.ds(2 * width, width)])
     copies.send(query, query_hbm)
     copies.finish()

time: 237 us -> 237 us (level)
  no operation moved by 1% of the time
where the time goes in v2:
time: 237 us; the launch traced here: 236 us
  Pallas kernels  123 us (52%)
  waiting for transfers between devices  51.6 us (22%)
  starting transfers between devices  29.7 us (13%)
  other arithmetic  26.3 us (11%)
  local copies, waits for them, and re-layouts  4.03 us (2%)
    pallas_call x15, Pallas kernels, call(): pl.pallas_call(kernel, out_shape=tuple(outs), in_specs=list(ins), out_spe...  123 us
    ppermute x20, waiting for transfers between devices, move(): self.parts.append(lax.ppermute(sent, ('row', 'tok'), pairs))  43.9 us
    convert_element_type x15, other arithmetic, next(): sent = sent.astype(self.parts[0].dtype)  26.3 us
    ppermute x20, starting transfers between devices, move(): self.parts.append(lax.ppermute(sent, ('row', 'tok'), pairs))  25.7 us
    ppermute x16, waiting for transfers between devices, swap_cores(): return lax.ppermute(array, 'tok', [(0, 1), (1, 0)])  7.73 us
  transfers between devices with their start and end apart: 36, of which 11 were waited for; matrix products, arithmetic and copies ran while one was open for 11% of the time, Pallas kernels for 35%

profile of v2, /device:TPU:0, one launch (start us, length us, event | category | flops | bytes accessed | tf_op | source)
XLA Modules:
  0.0 236.3 jit_solution(1088433758973066203)
XLA Ops:
  0.7 4.9 %shard_map.263 = (bf16[256,768]{1,0:T(8,128)(2,1)}, bf16[256,2688]{1,0:T(8,128)(2,1)}, bf16[256,384]{1,0:T(8,128)(2,1)}) custom-call(f32[2,768]{1,0:T(2,128)} %gain.9, f32[2,768]{1,0:T(2,128)} %next_shift.1, f32[2,2,768]{2,1,0:T(2,128)} %joint_bias.1, bf16[256,768]{1,0:T(8,128)(2,1)} %bitcast.4, bf16[2,768,2304]{2,1,0:T(8,128)(2,1)} %joint_hbm.5, ...), custom_call_target="tpu_custom_call" | custom-call | flops 905969664 | bytes 9854976 | tf_op jit(solution)/shard_map/pallas_call | solution.py:826
  6.2 2.5 %collective-permute-done.code_far = s32[1,256]{1,0:T(1,128)S(1)} collective-permute-done((s32[1,256]{1,0:T(1,128)S(1)}, s32[1,256]{1,0:T(1,128)S(1)}, u32[]{:S(2)}, u32[]{:S(2)}) %collective-permute-start) | collective-permute-done | bytes 1056 | tf_op jit(solution)/shard_map/ppermute | solution.py:838
  9.3 14.6 %shard_map.264 = (bf16[256,1536]{1,0:T(8,128)(2,1)}, bf16[256,3072]{1,0:T(8,128)(2,1)}, bf16[12,256,512]{2,1,0:T(8,128)(2,1)}, f32[256,768]{1,0:T(8,128)}, bf16[...) custom-call(s32[1,256]{1,0:T(1,128)} %copy-done.14, ...), custom_call_target="tpu_custom_call" | custom-call | flops 4026531840 | bytes 42149888 | tf_op jit(solution)/shard_map/pallas_call | solution.py:826
  24.3 2.9 %collective-permute-done.2.far_hbm.refs_4_ = bf16[256,2304]{1,0:T(8,128)(2,1)} collective-permute-done((bf16[256,2304]{1,0:T(8,128)(2,1)}, bf16[256,2304]{1,0:T(8,128)(2,1)}, u32[]{:S(2)}, u32[]{:S(2)}) %collective-permute-start.2) | collective-permute-done | bytes 1179680 | tf_op jit(solution)/shard_map/ppermute | solution.py:838
  27.2 17.8 %shard_map.265 = (bf16[256,1536]{1,0:T(8,128)(2,1)}, bf16[256,3072]{1,0:T(8,128)(2,1)}, bf16[12,256,512]{2,1,0:T(8,128)(2,1)}, bf16[256,768]{1,0:T(8,128)(2,1)},...) custom-call(s32[1,256]{1,0:T(1,128)} %copy-done.14, ...), custom_call_target="tpu_custom_call" | custom-call | flops 5536481280 | bytes 34383872 | tf_op jit(solution)/shard_map/pallas_call | solution.py:826
  45.9 10.5 %shard_map.266 = (bf16[256,768]{1,0:T(8,128)(2,1)}, f32[256,1536]{1,0:T(8,128)}, bf16[256,1536]{1,0:T(8,128)(2,1)}, f32[8,768]{1,0:T(8,128)}) custom-call(bf16[256,768]{1,0:T(8,128)(2,1)} %get-tuple-element.98.low_hbm, bf16[256,768]{1,0:T(8,128)(2,1)} %get-tuple-element.95.query_hbm, bf16[256,2304]{1,0:T(8,128)(2,1)} %get-tuple-element.96.packed_hbm.refs_3_, ...), custom_call_target="tpu_custom_call" | custom-call | flops 1308622848 | bytes 11427840 | tf_op jit(solution)/shard_map/pallas_call | solution.py:826
  57.0 6.3 %shard_map.267 = (bf16[8,192,384]{2,1,0:T(8,128)(2,1)}, bf16[8,192,384]{2,1,0:T(8,128)(2,1)}) custom-call(s32[1,256]{1,0:T(1,128)} %copy-done.14, bf16[256,3072]{1,0:T(8,128)(2,1)} %get-tuple-element.102.refs_1_, bf16[256,3072]{1,0:T(8,128)(2,1)} %collective-permute-done.3.refs_2_, bf16[256,384]{1,0:T(8,128)(2,1)} %get-tuple-element.103.refs_3_, ...), custom_call_target="tpu_custom_call" | custom-call | flops 1207959552 | bytes 7078912 | tf_op jit(solution)/shard_map/pallas_call | solution.py:826
  63.3 2.7 %collective-permute-start.7 = (bf16[8,192,384]{2,1,0:T(8,128)(2,1)}, bf16[8,192,384]{2,1,0:T(8,128)(2,1)}, u32[]{:S(2)}, u32[]{:S(2)}) collective-permute-start(bf16[8,192,384]{2,1,0:T(8,128)(2,1)} %get-tuple-element.119), channel_id=1, source_target_pairs={{0,2},{1,5},{2,0},{3,7},{4,6},{5,1},{6,4},{7,3},{8,10},{9,13},{10,... | collective-permute-start | bytes 3538952 | tf_op jit(solution)/shard_map/ppermute | solution.py:875
  66.1 6.3 %shard_map.268 = (bf16[8,240,384]{2,1,0:T(8,128)(2,1)}, bf16[8,240,384]{2,1,0:T(8,128)(2,1)}) custom-call(s32[1,256]{1,0:T(1,128)} %copy-done.14, bf16[256,1536]{1,0:T(8,128)(2,1)} %get-tuple-element.106.refs_1_, bf16[256,1536]{1,0:T(8,128)(2,1)} %collective-permute-done.4.refs_2_, bf16[256,1920]{1,0:T(8,128)(2,1)} %get-tuple-element.107.refs_3_, ...), custom_call_target="tpu_custom_call" | custom-call | flops 1509949440 | bytes 6489088 | tf_op jit(solution)/shard_map/pallas_call | solution.py:826
  73.4 14.3 %shard_map.269 = (bf16[256,1152]{1,0:T(8,128)(2,1)}, bf16[256,1152]{1,0:T(8,128)(2,1)}, bf16[256,384]{1,0:T(8,128)(2,1)}, bf16[256,384]{1,0:T(8,128)(2,1)}, bf16...) custom-call(s32[1,256]{1,0:T(1,128)} %copy-done.14, ...), custom_call_target="tpu_custom_call" | custom-call | flops 3321888768 | bytes 37565440 | tf_op jit(solution)/shard_map/pallas_call | solution.py:826
  88.4 2.2 add_convert_fusion.3
  91.9 10.0 %shard_map.270 = (bf16[8,352,384]{2,1,0:T(8,128)(2,1)}, bf16[8,352,384]{2,1,0:T(8,128)(2,1)}) custom-call(s32[1,256]{1,0:T(1,128)} %copy-done.14, f32[8,768]{1,0:T(8,128)} %get-tuple-element.121.refs_1_, f32[8,3072]{1,0:T(8,128)} %get-tuple-element.122.refs_2_, bf16[256,2304]{1,0:T(8,128)(2,1)} %get-tuple-element.96.packed_hbm.refs_3_, ...), custom_call_target="tpu_custom_call" | custom-call | flops 2113929216 | bytes 11527168 | tf_op jit(solution)/shard_map/pallas_call | solution.py:826
  101.9 2.0 collective-permute-start.21
  105.5 2.5 %add_convert_fusion.2 = bf16[4,240,384]{2,1,0:T(8,128)(2,1)} fusion(bf16[8,240,384]{2,1,0:T(8,128)(2,1)} %collective-permute-done.11.refs_6_, bf16[8,240,384]{2,1,0:T(8,128)(2,1)} %get-tuple-element.109.refs_5_), kind=kLoop, calls=%fused_computation.2 | loop fusion | flops 1474560 | bytes 2211840 | tf_op jit(solution)/shard_map/convert_element_type | solution.py:881
  108.4 6.3 %shard_map.271 = (bf16[8,240,384]{2,1,0:T(8,128)(2,1)}, bf16[8,240,384]{2,1,0:T(8,128)(2,1)}) custom-call(s32[1,256]{1,0:T(1,128)} %copy-done.14, bf16[256,1536]{1,0:T(8,128)(2,1)} %get-tuple-element.131.refs_1_, bf16[256,1536]{1,0:T(8,128)(2,1)} %collective-permute-done.12.refs_2_, bf16[256,1920]{1,0:T(8,128)(2,1)} %get-tuple-element.132.refs_3_, ...), custom_call_target="tpu_custom_call" | custom-call | flops 1509949440 | bytes 6489088 | tf_op jit(solution)/shard_map/pallas_call | solution.py:826
  114.9 5.5 %collective-permute-done.14.refs_2_ = bf16[4,192,384]{2,1,0:T(8,128)(2,1)} collective-permute-done((bf16[4,192,384]{2,1,0:T(8,128)(2,1)}, bf16[4,192,384]{2,1,0:T(8,128)(2,1)}, u32[]{:S(2)}, u32[]{:S(2)}) %collective-permute-start.14) | collective-permute-done | bytes 589856 | tf_op jit(solution)/shard_map/ppermute | solution.py:875
  120.5 2.0 add_convert_fusion.8
  124.0 10.5 %shard_map.272 = (bf16[256,768]{1,0:T(8,128)(2,1)}, f32[256,1536]{1,0:T(8,128)}, bf16[256,1536]{1,0:T(8,128)(2,1)}, f32[8,768]{1,0:T(8,128)}) custom-call(bf16[256,768]{1,0:T(8,128)(2,1)} %get-tuple-element.135.low_hbm, bf16[256,768]{1,0:T(8,128)(2,1)} %get-tuple-element.92.query_hbm, bf16[256,2688]{1,0:T(8,128)(2,1)} %get-tuple-element.93.packed_hbm.refs_3_, ...), custom_call_target="tpu_custom_call" | custom-call | flops 1308622848 | bytes 11821056 | tf_op jit(solution)/shard_map/pallas_call | solution.py:826
  136.4 2.2 add_convert_fusion.7
  139.1 7.2 %shard_map.273 = (bf16[256,1152]{1,0:T(8,128)(2,1)}, bf16[256,1152]{1,0:T(8,128)(2,1)}, f32[256,768]{1,0:T(8,128)}, f32[8,768]{1,0:T(8,128)}) custom-call(s32[1,256]{1,0:T(1,128)} %copy-done.14, f32[2,768]{1,0:T(2,128)} %gain.9, f32[8,768]{1,0:T(8,128)} %get-tuple-element.139.dq_sum, f32[8,768]{1,0:T(8,128)} %get-tuple-element.140.vectors_two, ...), custom_call_target="tpu_custom_call" | custom-call | flops 905969664 | bytes 13057024 | tf_op jit(solution)/shard_map/pallas_call | solution.py:826
  146.7 3.0 %add_convert_fusion = bf16[4,352,384]{2,1,0:T(8,128)(2,1)} fusion(bf16[8,352,384]{2,1,0:T(8,128)(2,1)} %collective-permute-done.21.refs_11_, bf16[8,352,384]{2,1,0:T(8,128)(2,1)} %get-tuple-element.128.refs_10_), kind=kLoop, calls=%fused_computation | loop fusion | flops 2162688 | bytes 3244032 | tf_op jit(solution)/shard_map/convert_element_type | solution.py:881
  153.0 2.3 add_convert_fusion.1
  155.3 6.0 %shard_map.275 = (bf16[8,160,384]{2,1,0:T(8,128)(2,1)}, bf16[8,160,384]{2,1,0:T(8,128)(2,1)}) custom-call(s32[1,256]{1,0:T(1,128)} %copy-done.14, f32[8,768]{1,0:T(8,128)} %get-tuple-element.150.refs_1_, f32[8,3072]{1,0:T(8,128)} %get-tuple-element.151.refs_2_, bf16[256,2688]{1,0:T(8,128)(2,1)} %get-tuple-element.93.packed_hbm.refs_3_, ...), custom_call_target="tpu_custom_call" | custom-call | flops 905969664 | bytes 6022144 | tf_op jit(solution)/shard_map/pallas_call | solution.py:826
  163.7 12.2 %collective-permute-done.22.refs_12_ = bf16[4,352,384]{2,1,0:T(8,128)(2,1)} collective-permute-done((bf16[4,352,384]{2,1,0:T(8,128)(2,1)}, bf16[4,352,384]{2,1,0:T(8,128)(2,1)}, u32[]{:S(2)}, u32[]{:S(2)}) %collective-permute-start.22) | collective-permute-done | bytes 1081376 | tf_op jit(solution)/shard_map/ppermute | solution.py:875
  179.0 2.6 %collective-permute-start.18 = (bf16[1,192,384]{2,1,0:T(8,128)(2,1)S(1)}, bf16[1,192,384]{2,1,0:T(8,128)(2,1)S(1)}, u32[]{:S(2)}, u32[]{:S(2)}) collective-permute-start(bf16[1,192,384]{2,1,0:T(8,128)(2,1)S(1)} %copy-done.11), channel_id=1, source_target_pairs={{0,16},{1,17},{2,18},{3,19},{4,20},{5,21},{6,22},{7,23},{8,24},{9,... | collective-permute-start | bytes 442376 | tf_op jit(solution)/shard_map/ppermute | solution.py:875
  182.0 4.0 %collective-permute-done.31.refs_6_ = bf16[8,160,384]{2,1,0:T(8,128)(2,1)S(1)} collective-permute-done((bf16[8,160,384]{2,1,0:T(8,128)(2,1)}, bf16[8,160,384]{2,1,0:T(8,128)(2,1)S(1)}, u32[]{:S(2)}, u32[]{:S(2)}) %collective-permute-start.31) | collective-permute-done | bytes 983072 | tf_op jit(solution)/shard_map/ppermute | solution.py:875
  190.6 2.7 %collective-permute-start.24 = (bf16[1,352,384]{2,1,0:T(8,128)(2,1)S(1)}, bf16[1,352,384]{2,1,0:T(8,128)(2,1)}, u32[]{:S(2)}, u32[]{:S(2)}) collective-permute-start(bf16[1,352,384]{2,1,0:T(8,128)(2,1)S(1)} %add_convert_fusion.9), channel_id=1, source_target_pairs={{0,16},{1,17},{2,18},{3,19},{4,20},{5,21},{6,22},{7,23},{8,24},{9,... | collective-permute-start | bytes 811016 | tf_op jit(solution)/shard_map/ppermute | solution.py:875
  197.0 12.4 %collective-permute-done.28.refs_3_ = bf16[2,240,384]{2,1,0:T(8,128)(2,1)S(1)} collective-permute-done((bf16[2,240,384]{2,1,0:T(8,128)(2,1)S(1)}, bf16[2,240,384]{2,1,0:T(8,128)(2,1)S(1)}, u32[]{:S(2)}, u32[]{:S(2)}) %collective-permute-start.28) | collective-permute-done | bytes 368672 | tf_op jit(solution)/shard_map/ppermute | solution.py:875
  213.6 3.4 %shard_map.274 = (f32[400,384]{1,0:T(8,128)}, f32[400,384]{1,0:T(8,128)}) custom-call(bf16[8,192,384]{2,1,0:T(8,128)(2,1)} %get-tuple-element.104.refs_0_, bf16[8,192,384]{2,1,0:T(8,128)(2,1)} %collective-permute-done.7.refs_1_, bf16[4,192,384]{2,1,0:T(8,128)(2,1)} %collective-permute-done.14.refs_2_, bf16[2,192,384]{2,1,0:T(8,128)(2,1)} %collective-permute-done.15.refs_3_, ...), custom_call_target="tpu_custom_call" | custom-call | bytes 15077376 | tf_op jit(solution)/shard_map/pallas_call | solution.py:826
  220.4 7.1 %collective-permute-done.34.refs_9_ = bf16[1,160,384]{2,1,0:T(8,128)(2,1)S(1)} collective-permute-done((bf16[1,160,384]{2,1,0:T(8,128)(2,1)S(1)}, bf16[1,160,384]{2,1,0:T(8,128)(2,1)S(1)}, u32[]{:S(2)}, u32[]{:S(2)}) %collective-permute-start.34) | collective-permute-done | bytes 122912 | tf_op jit(solution)/shard_map/ppermute | solution.py:875
  228.2 2.6 %shard_map.276 = (f32[208,384]{1,0:T(8,128)}, f32[208,384]{1,0:T(8,128)}) custom-call(bf16[8,240,384]{2,1,0:T(8,128)(2,1)} %get-tuple-element.134.refs_0_, bf16[8,240,384]{2,1,0:T(8,128)(2,1)} %collective-permute-done.26.refs_1_, bf16[4,240,384]{2,1,0:T(8,128)(2,1)} %copy-done.3, bf16[2,240,384]{2,1,0:T(8,128)(2,1)} %copy-done.7, ...), custom_call_target="tpu_custom_call" | custom-call | bytes 7704576 | tf_op jit(solution)/shard_map/pallas_call | solution.py:826
  233.4 2.7 %shard_map.277 = (f32[2,24,2304]{2,1,0:T(8,128)}, f32[2,24,768]{2,1,0:T(8,128)}, f32[2,24,3072]{2,1,0:T(8,128)}, f32[2,96,768]{2,1,0:T(8,128)}, f32[2,24]{1,0:T(...) custom-call(f32[400,384]{1,0:T(8,128)} %get-tuple-element.146.refs_0, ...), custom_call_target="tpu_custom_call" | custom-call | bytes 3639552 | tf_op jit(solution)/shard_map/pallas_call | solution.py:826
  (111 shorter events, 40.8 us)
Async XLA Ops:
  5.6 3.6 %collective-permute-start.1 = (bf16[256,2688]{1,0:T(8,128)(2,1)}, bf16[256,2688]{1,0:T(8,128)(2,1)}, u32[]{:S(2)}, u32[]{:S(2)}) collective-permute-start(bf16[256,2688]{1,0:T(8,128)(2,1)} %get-tuple-element.93.packed_hbm.refs_3_), channel_id=1, source_target_pairs={{0,1},{1,0},{2,3},{3,2},{4,5},{5,4},{6,7},{7,6},{8,9},{9,8},{10,11... | collective-permute-start | bytes 4128776 | tf_op jit(solution)/shard_map/ppermute | solution.py:838
  45.0 12.0 %collective-permute-start.3 = (bf16[256,3072]{1,0:T(8,128)(2,1)}, bf16[256,3072]{1,0:T(8,128)(2,1)}, u32[]{:S(2)}, u32[]{:S(2)}) collective-permute-start(bf16[256,3072]{1,0:T(8,128)(2,1)} %get-tuple-element.102.refs_1_), channel_id=1, source_target_pairs={{0,1},{1,0},{2,3},{3,2},{4,5},{5,4},{6,7},{7,6},{8,9},{9,8},{10,11... | collective-permute-start | bytes 4718600 | tf_op jit(solution)/shard_map/ppermute | solution.py:838
  45.4 20.7 %collective-permute-start.5 = (bf16[256,1920]{1,0:T(8,128)(2,1)}, bf16[256,1920]{1,0:T(8,128)(2,1)}, u32[]{:S(2)}, u32[]{:S(2)}) collective-permute-start(bf16[256,1920]{1,0:T(8,128)(2,1)} %get-tuple-element.108), channel_id=1, source_target_pairs={{0,1},{1,0},{2,3},{3,2},{4,5},{5,4},{6,7},{7,6},{8,9},{9,8},{10,11... | collective-permute-start | bytes 2949128 | tf_op jit(solution)/shard_map/ppermute | solution.py:838
  45.6 20.4 %collective-permute-start.4 = (bf16[256,1536]{1,0:T(8,128)(2,1)}, bf16[256,1536]{1,0:T(8,128)(2,1)}, u32[]{:S(2)}, u32[]{:S(2)}) collective-permute-start(bf16[256,1536]{1,0:T(8,128)(2,1)} %get-tuple-element.106.refs_1_), channel_id=1, source_target_pairs={{0,1},{1,0},{2,3},{3,2},{4,5},{5,4},{6,7},{7,6},{8,9},{9,8},{10,11... | collective-permute-start | bytes 2359304 | tf_op jit(solution)/shard_map/ppermute | solution.py:838
  56.4 16.0 %collective-permute-start.6 = (bf16[256,1536]{1,0:T(8,128)(2,1)}, bf16[256,1536]{1,0:T(8,128)(2,1)S(1)}, u32[]{:S(2)}, u32[]{:S(2)}) collective-permute-start(bf16[256,1536]{1,0:T(8,128)(2,1)} %get-tuple-element.114), channel_id=1, source_target_pairs={{0,1},{1,0},{2,3},{3,2},{4,5},{5,4},{6,7},{7,6},{8,9},{9,8},{10,11... | collective-permute-start | bytes 2359304 | tf_op jit(solution)/shard_map/ppermute | solution.py:838
  56.7 33.9 %collective-permute-start.9 = (bf16[256,3072]{1,0:T(8,128)(2,1)}, bf16[256,3072]{1,0:T(8,128)(2,1)}, u32[]{:S(2)}, u32[]{:S(2)}) collective-permute-start(bf16[256,3072]{1,0:T(8,128)(2,1)} %get-tuple-element.125.refs_7_), channel_id=1, source_target_pairs={{0,1},{1,0},{2,3},{3,2},{4,5},{5,4},{6,7},{7,6},{8,9},{9,8},{10,11... | collective-permute-start | bytes 4718600 | tf_op jit(solution)/shard_map/ppermute | solution.py:838
  63.3 25.0 %collective-permute-start.7 = (bf16[8,192,384]{2,1,0:T(8,128)(2,1)}, bf16[8,192,384]{2,1,0:T(8,128)(2,1)}, u32[]{:S(2)}, u32[]{:S(2)}) collective-permute-start(bf16[8,192,384]{2,1,0:T(8,128)(2,1)} %get-tuple-element.119), channel_id=1, source_target_pairs={{0,2},{1,5},{2,0},{3,7},{4,6},{5,1},{6,4},{7,3},{8,10},{9,13},{10,... | collective-permute-start | bytes 3538952 | tf_op jit(solution)/shard_map/ppermute | solution.py:875
  72.3 33.1 %collective-permute-start.11 = (bf16[8,240,384]{2,1,0:T(8,128)(2,1)}, bf16[8,240,384]{2,1,0:T(8,128)(2,1)}, u32[]{:S(2)}, u32[]{:S(2)}) collective-permute-start(bf16[8,240,384]{2,1,0:T(8,128)(2,1)} %get-tuple-element.129), channel_id=1, source_target_pairs={{0,2},{1,5},{2,0},{3,7},{4,6},{5,1},{6,4},{7,3},{8,10},{9,13},{10,... | collective-permute-start | bytes 4423688 | tf_op jit(solution)/shard_map/ppermute | solution.py:875
  87.7 3.3 %collective-permute-start.8 = (bf16[256,1152]{1,0:T(8,128)(2,1)}, bf16[256,1152]{1,0:T(8,128)(2,1)S(1)}, u32[]{:S(2)}, u32[]{:S(2)}) collective-permute-start(bf16[256,1152]{1,0:T(8,128)(2,1)} %get-tuple-element.124), channel_id=1, source_target_pairs={{0,1},{1,0},{2,3},{3,2},{4,5},{5,4},{6,7},{7,6},{8,9},{9,8},{10,11... | collective-permute-start | bytes 1769480 | tf_op jit(solution)/shard_map/ppermute | solution.py:838
  88.3 20.1 %collective-permute-start.13 = (bf16[256,1920]{1,0:T(8,128)(2,1)}, bf16[256,1920]{1,0:T(8,128)(2,1)}, u32[]{:S(2)}, u32[]{:S(2)}) collective-permute-start(bf16[256,1920]{1,0:T(8,128)(2,1)} %get-tuple-element.133), channel_id=1, source_target_pairs={{0,1},{1,0},{2,3},{3,2},{4,5},{5,4},{6,7},{7,6},{8,9},{9,8},{10,11... | collective-permute-start | bytes 2949128 | tf_op jit(solution)/shard_map/ppermute | solution.py:838
  90.6 17.8 %collective-permute-start.12 = (bf16[256,1536]{1,0:T(8,128)(2,1)}, bf16[256,1536]{1,0:T(8,128)(2,1)}, u32[]{:S(2)}, u32[]{:S(2)}) collective-permute-start(bf16[256,1536]{1,0:T(8,128)(2,1)} %get-tuple-element.131.refs_1_), channel_id=1, source_target_pairs={{0,1},{1,0},{2,3},{3,2},{4,5},{5,4},{6,7},{7,6},{8,9},{9,8},{10,11... | collective-permute-start | bytes 2359304 | tf_op jit(solution)/shard_map/ppermute | solution.py:838
  101.9 44.8 %collective-permute-start.21 = (bf16[8,352,384]{2,1,0:T(8,128)(2,1)}, bf16[8,352,384]{2,1,0:T(8,128)(2,1)}, u32[]{:S(2)}, u32[]{:S(2)}) collective-permute-start(bf16[8,352,384]{2,1,0:T(8,128)(2,1)} %get-tuple-element.145), channel_id=1, source_target_pairs={{0,2},{1,5},{2,0},{3,7},{4,6},{5,1},{6,4},{7,3},{8,10},{9,13},{10,... | collective-permute-start | bytes 6488072 | tf_op jit(solution)/shard_map/ppermute | solution.py:875
  103.9 16.5 %collective-permute-start.14 = (bf16[4,192,384]{2,1,0:T(8,128)(2,1)}, bf16[4,192,384]{2,1,0:T(8,128)(2,1)}, u32[]{:S(2)}, u32[]{:S(2)}) collective-permute-start(bf16[4,192,384]{2,1,0:T(8,128)(2,1)} %add_convert_fusion.3), channel_id=1, source_target_pairs={{0,8},{1,9},{2,10},{3,11},{4,12},{5,13},{6,14},{7,15},{8,0},{9,1},... | collective-permute-start | bytes 1769480 | tf_op jit(solution)/shard_map/ppermute | solution.py:875
  107.9 28.5 %collective-permute-start.16 = (bf16[4,240,384]{2,1,0:T(8,128)(2,1)}, bf16[4,240,384]{2,1,0:T(8,128)(2,1)S(1)}, u32[]{:S(2)}, u32[]{:S(2)}) collective-permute-start(bf16[4,240,384]{2,1,0:T(8,128)(2,1)} %add_convert_fusion.2), channel_id=1, source_target_pairs={{0,8},{1,9},{2,10},{3,11},{4,12},{5,13},{6,14},{7,15},{8,0},{9,1},... | collective-permute-start | bytes 2211848 | tf_op jit(solution)/shard_map/ppermute | solution.py:875
  114.8 38.3 %collective-permute-start.26 = (bf16[8,240,384]{2,1,0:T(8,128)(2,1)}, bf16[8,240,384]{2,1,0:T(8,128)(2,1)}, u32[]{:S(2)}, u32[]{:S(2)}) collective-permute-start(bf16[8,240,384]{2,1,0:T(8,128)(2,1)} %get-tuple-element.148), channel_id=1, source_target_pairs={{0,2},{1,5},{2,0},{3,7},{4,6},{5,1},{6,4},{7,3},{8,10},{9,13},{10,... | collective-permute-start | bytes 4423688 | tf_op jit(solution)/shard_map/ppermute | solution.py:875
  122.4 12.1 %collective-permute-start.15 = (bf16[2,192,384]{2,1,0:T(8,128)(2,1)}, bf16[2,192,384]{2,1,0:T(8,128)(2,1)}, u32[]{:S(2)}, u32[]{:S(2)}) collective-permute-start(bf16[2,192,384]{2,1,0:T(8,128)(2,1)} %add_convert_fusion.8), channel_id=1, source_target_pairs={{0,4},{1,3},{2,6},{3,1},{4,0},{5,7},{6,2},{7,5},{8,12},{9,11},{10,... | collective-permute-start | bytes 884744 | tf_op jit(solution)/shard_map/ppermute | solution.py:875
  134.5 4.7 %collective-permute-start.17 = (bf16[256,1536]{1,0:T(8,128)(2,1)}, bf16[256,1536]{1,0:T(8,128)(2,1)}, u32[]{:S(2)}, u32[]{:S(2)}) collective-permute-start(bf16[256,1536]{1,0:T(8,128)(2,1)} %get-tuple-element.142), channel_id=1, source_target_pairs={{0,1},{1,0},{2,3},{3,2},{4,5},{5,4},{6,7},{7,6},{8,9},{9,8},{10,11... | collective-permute-start | bytes 2359304 | tf_op jit(solution)/shard_map/ppermute | solution.py:838
  138.7 12.5 %collective-permute-start.19 = (bf16[2,240,384]{2,1,0:T(8,128)(2,1)}, bf16[2,240,384]{2,1,0:T(8,128)(2,1)}, u32[]{:S(2)}, u32[]{:S(2)}) collective-permute-start(bf16[2,240,384]{2,1,0:T(8,128)(2,1)} %add_convert_fusion.7), channel_id=1, source_target_pairs={{0,4},{1,3},{2,6},{3,1},{4,0},{5,7},{6,2},{7,5},{8,12},{9,11},{10,... | collective-permute-start | bytes 1105928 | tf_op jit(solution)/shard_map/ppermute | solution.py:875
  146.3 8.9 %collective-permute-start.30 = (bf16[256,1152]{1,0:T(8,128)(2,1)}, bf16[256,1152]{1,0:T(8,128)(2,1)}, u32[]{:S(2)}, u32[]{:S(2)}) collective-permute-start(bf16[256,1152]{1,0:T(8,128)(2,1)} %get-tuple-element.153), channel_id=1, source_target_pairs={{0,1},{1,0},{2,3},{3,2},{4,5},{5,4},{6,7},{7,6},{8,9},{9,8},{10,11... | collective-permute-start | bytes 1769480 | tf_op jit(solution)/shard_map/ppermute | solution.py:838
  149.6 26.3 %collective-permute-start.22 = (bf16[4,352,384]{2,1,0:T(8,128)(2,1)}, bf16[4,352,384]{2,1,0:T(8,128)(2,1)}, u32[]{:S(2)}, u32[]{:S(2)}) collective-permute-start(bf16[4,352,384]{2,1,0:T(8,128)(2,1)} %add_convert_fusion), channel_id=1, source_target_pairs={{0,8},{1,9},{2,10},{3,11},{4,12},{5,13},{6,14},{7,15},{8,0},{9,1},... | collective-permute-start | bytes 3244040 | tf_op jit(solution)/shard_map/ppermute | solution.py:875
  161.3 24.7 %collective-permute-start.31 = (bf16[8,160,384]{2,1,0:T(8,128)(2,1)}, bf16[8,160,384]{2,1,0:T(8,128)(2,1)S(1)}, u32[]{:S(2)}, u32[]{:S(2)}) collective-permute-start(bf16[8,160,384]{2,1,0:T(8,128)(2,1)} %get-tuple-element.155), channel_id=1, source_target_pairs={{0,2},{1,5},{2,0},{3,7},{4,6},{5,1},{6,4},{7,3},{8,10},{9,13},{10,... | collective-permute-start | bytes 2949128 | tf_op jit(solution)/shard_map/ppermute | solution.py:875
  162.8 24.7 %collective-permute-start.27 = (bf16[4,240,384]{2,1,0:T(8,128)(2,1)}, bf16[4,240,384]{2,1,0:T(8,128)(2,1)S(1)}, u32[]{:S(2)}, u32[]{:S(2)}) collective-permute-start(bf16[4,240,384]{2,1,0:T(8,128)(2,1)} %add_convert_fusion.1), channel_id=1, source_target_pairs={{0,4},{1,3},{2,6},{3,1},{4,0},{5,7},{6,2},{7,5},{8,12},{9,11},{10,... | collective-permute-start | bytes 2211848 | tf_op jit(solution)/shard_map/ppermute | solution.py:875
  177.5 11.6 %collective-permute-start.23 = (bf16[2,352,384]{2,1,0:T(8,128)(2,1)S(1)}, bf16[2,352,384]{2,1,0:T(8,128)(2,1)S(1)}, u32[]{:S(2)}, u32[]{:S(2)}) collective-permute-start(bf16[2,352,384]{2,1,0:T(8,128)(2,1)S(1)} %add_convert_fusion.4), channel_id=1, source_target_pairs={{0,4},{1,3},{2,6},{3,1},{4,0},{5,7},{6,2},{7,5},{8,12},{9,11},{10,... | collective-permute-start | bytes 1622024 | tf_op jit(solution)/shard_map/ppermute | solution.py:875
  179.0 33.9 %collective-permute-start.18 = (bf16[1,192,384]{2,1,0:T(8,128)(2,1)S(1)}, bf16[1,192,384]{2,1,0:T(8,128)(2,1)S(1)}, u32[]{:S(2)}, u32[]{:S(2)}) collective-permute-start(bf16[1,192,384]{2,1,0:T(8,128)(2,1)S(1)} %copy-done.11), channel_id=1, source_target_pairs={{0,16},{1,17},{2,18},{3,19},{4,20},{5,21},{6,22},{7,23},{8,24},{9,... | collective-permute-start | bytes 442376 | tf_op jit(solution)/shard_map/ppermute | solution.py:875
  181.7 31.3 %collective-permute-start.20 = (bf16[1,240,384]{2,1,0:T(8,128)(2,1)S(1)}, bf16[1,240,384]{2,1,0:T(8,128)(2,1)}, u32[]{:S(2)}, u32[]{:S(2)}) collective-permute-start(bf16[1,240,384]{2,1,0:T(8,128)(2,1)S(1)} %copy-done.10), channel_id=1, source_target_pairs={{0,16},{1,17},{2,18},{3,19},{4,20},{5,21},{6,22},{7,23},{8,24},{9,... | collective-permute-start | bytes 552968 | tf_op jit(solution)/shard_map/ppermute | solution.py:875
  186.1 8.9 %collective-permute-start.32 = (bf16[4,160,384]{2,1,0:T(8,128)(2,1)S(1)}, bf16[4,160,384]{2,1,0:T(8,128)(2,1)S(1)}, u32[]{:S(2)}, u32[]{:S(2)}) collective-permute-start(bf16[4,160,384]{2,1,0:T(8,128)(2,1)S(1)} %add_convert_fusion.5), channel_id=1, source_target_pairs={{0,4},{1,3},{2,6},{3,1},{4,0},{5,7},{6,2},{7,5},{8,12},{9,11},{10,... | collective-permute-start | bytes 1474568 | tf_op jit(solution)/shard_map/ppermute | solution.py:875
  189.0 20.4 %collective-permute-start.28 = (bf16[2,240,384]{2,1,0:T(8,128)(2,1)S(1)}, bf16[2,240,384]{2,1,0:T(8,128)(2,1)S(1)}, u32[]{:S(2)}, u32[]{:S(2)}) collective-permute-start(bf16[2,240,384]{2,1,0:T(8,128)(2,1)S(1)} %add_convert_fusion.6), channel_id=1, source_target_pairs={{0,8},{1,9},{2,10},{3,11},{4,12},{5,13},{6,14},{7,15},{8,0},{9,1},... | collective-permute-start | bytes 1105928 | tf_op jit(solution)/shard_map/ppermute | solution.py:875
  190.6 23.0 %collective-permute-start.24 = (bf16[1,352,384]{2,1,0:T(8,128)(2,1)S(1)}, bf16[1,352,384]{2,1,0:T(8,128)(2,1)}, u32[]{:S(2)}, u32[]{:S(2)}) collective-permute-start(bf16[1,352,384]{2,1,0:T(8,128)(2,1)S(1)} %add_convert_fusion.9), channel_id=1, source_target_pairs={{0,16},{1,17},{2,18},{3,19},{4,20},{5,21},{6,22},{7,23},{8,24},{9,... | collective-permute-start | bytes 811016 | tf_op jit(solution)/shard_map/ppermute | solution.py:875
  195.9 21.2 %collective-permute-start.33 = (bf16[2,160,384]{2,1,0:T(8,128)(2,1)}, bf16[2,160,384]{2,1,0:T(8,128)(2,1)}, u32[]{:S(2)}, u32[]{:S(2)}) collective-permute-start(bf16[2,160,384]{2,1,0:T(8,128)(2,1)} %add_convert_fusion.10), channel_id=1, source_target_pairs={{0,8},{1,9},{2,10},{3,11},{4,12},{5,13},{6,14},{7,15},{8,0},{9,1},... | collective-permute-start | bytes 737288 | tf_op jit(solution)/shard_map/ppermute | solution.py:875
  211.3 9.1 %collective-permute-start.29 = (bf16[1,240,384]{2,1,0:T(8,128)(2,1)}, bf16[1,240,384]{2,1,0:T(8,128)(2,1)}, u32[]{:S(2)}, u32[]{:S(2)}) collective-permute-start(bf16[1,240,384]{2,1,0:T(8,128)(2,1)} %add_convert_fusion.11), channel_id=1, source_target_pairs={{0,16},{1,17},{2,18},{3,19},{4,20},{5,21},{6,22},{7,23},{8,24},{9,... | collective-permute-start | bytes 552968 | tf_op jit(solution)/shard_map/ppermute | solution.py:875
  217.0 15.6 %collective-permute-start.25 = (f32[400,384]{1,0:T(8,128)}, f32[400,384]{1,0:T(8,128)}, u32[]{:S(2)}, u32[]{:S(2)}) collective-permute-start(f32[400,384]{1,0:T(8,128)} %get-tuple-element.147), channel_id=1, source_target_pairs={{0,1},{1,0},{2,3},{3,2},{4,5},{5,4},{6,7},{7,6},{8,9},{9,8},{10,11... | collective-permute-start | bytes 1843208 | tf_op jit(solution)/shard_map/ppermute | solution.py:838
  218.2 9.3 %collective-permute-start.34 = (bf16[1,160,384]{2,1,0:T(8,128)(2,1)S(1)}, bf16[1,160,384]{2,1,0:T(8,128)(2,1)S(1)}, u32[]{:S(2)}, u32[]{:S(2)}) collective-permute-start(bf16[1,160,384]{2,1,0:T(8,128)(2,1)S(1)} %add_convert_fusion.14), channel_id=1, source_target_pairs={{0,16},{1,17},{2,18},{3,19},{4,20},{5,21},{6,22},{7,23},{8,24},{9,... | collective-permute-start | bytes 368648 | tf_op jit(solution)/shard_map/ppermute | solution.py:875
  (24 other events, 187.3 us)
